TPU v7x, 256 devices: a whole 4x4x8 slice. The times are simulated.
256 devices in a mesh: vocab: 32 (over x, z), prange: 4 (over y), query: 2 (over core).
Axes of the slice: x: 4, y: 4, z: 8, core: 2. Of those that a mesh axis runs over, the one named last changes fastest.
Arguments:
- term_ids: int32 [4096, 32], P('query'), may hold values from 0 to 32767
- term_weights: bfloat16 [4096, 32], P('query'), may hold values from 0.049804688 to 1
- impact: bfloat16 [32768, 8192], P('vocab', 'prange'), may hold values from 0.0099487305 to 1
- query_rows: bfloat16 [128, 32768], P(('prange', 'query'), 'vocab'), may hold values from -0.3125 to 0.3125
- candidates: int32 [128, 4], P(('prange', 'query')), may hold values from 0 to 63, all different within a row; in each aligned block of 16 rows (0 to 15, 16 to 31, ...) at most 2 rows name the same one
Outputs:
- first_scores: bfloat16 [4, 2048, 4096], P('prange', 'vocab', 'query')
- rescored: float32 [128, 4, 128], P(('prange', 'query'), None, 'vocab')
Inputs may be any that keep to these rules, and one draw needn't show every extreme that they name: `candidates`: each row names 4 different blocks. The 16 rows held by one device name any block at most 2 times, and some block exactly 2 times.
All inputs are finite; a program needn't handle non-finite values.
Results may differ from a plain program's by a relative error of at most 0.019.
Values may be sent and summed in bfloat16 or wider, within the bound.
No kernel may reach another device: no remote copies, remote signals or barrier semaphores. Data moves between devices by JAX's collectives and lax.ppermute only.
A program may use at most 64 MiB of HBM per device.

v0:
```python
import functools

import jax
import jax.numpy as jnp
from jax import lax
from jax.experimental import pallas as pl
from jax.experimental.pallas import tpu as pltpu
from jax.sharding import Mesh
from jax.sharding import PartitionSpec as P


BLOCK = 128
CANDS = 4
NX = 4
NZ = 8
NY = 4
LANES = 128
GROUP = 8
FIRST = 256
CHUNKS = 2
UNROLL = 32
CUTS = 16
F32 = jnp.float32
BF16 = jnp.bfloat16


def shifted(array, axis, shift):
    size = lax.axis_size(axis)
    return lax.ppermute(array, axis, [(i, (i + shift) % size) for i in range(size)])


def kept_in_hbm(array):
    return pltpu.with_memory_space_constraint(array, pltpu.HBM)


def dense_kernel(pos_ref, ids_ref, weights_ref, dense_ref, turned_ref, low_ref, key_ref, weight_ref, *, first):
    x, z, core = pos_ref[0], pos_ref[1], pos_ref[2]
    terms, queries = ids_ref.shape[0], dense_ref.shape[0]
    groups, pairs = low_ref.shape
    highs = dense_ref.shape[1] // FIRST
    ids = ids_ref[:, first : first + queries]
    x_rel = ((ids >> 13) - x) & (NX - 1)
    half_rel = ((ids >> 9) & 1) ^ core
    high = x_rel * 4 + half_rel * 2 + ((ids >> 8) & 1)
    key = high * GROUP + (lax.broadcasted_iota(jnp.int32, ids.shape, 1) & (GROUP - 1))
    key = jnp.where(((ids >> 10) & (NZ - 1)) == z, key, -1)
    low = (ids & (FIRST - 1)).astype(F32)
    weights = weights_ref[:, first : first + queries].astype(F32)
    turned_ref[...] = jnp.concatenate([low, key.astype(F32), weights, weights], axis=0).T
    place = lax.broadcasted_iota(jnp.int32, (groups, LANES), 1) // terms
    across = LANES // terms
    for kind, to_ref in enumerate((low_ref, key_ref, weight_ref)):
        for side in range(pairs // LANES):
            row = None
            for j in range(across):
                part = turned_ref[pl.ds(side * across + j, groups, stride=GROUP), :]
                shift = (terms * (j - kind)) % LANES
                part = pltpu.roll(part, shift, 1) if shift else part
                row = part if row is None else jnp.where(place == j, part, row)
            to_ref[:, side * LANES : (side + 1) * LANES] = row
    low_rows = lax.broadcasted_iota(jnp.int32, (FIRST, pairs), 0).astype(F32).astype(BF16)
    key_rows = lax.broadcasted_iota(jnp.int32, (highs * GROUP, pairs), 0).astype(F32).astype(BF16)
    one = jnp.ones((), BF16)
    zero = jnp.zeros((), BF16)

    def one_group(g):
        low = low_ref[pl.ds(g, 1), :].astype(BF16)
        keys = key_ref[pl.ds(g, 1), :].astype(BF16)
        weights = weight_ref[pl.ds(g, 1), :].astype(BF16)
        ones = jnp.where(low_rows == low, one, zero)
        spread = jnp.where(key_rows == keys, weights, zero)
        made = lax.dot_general(spread, ones, (((1,), (1,)), ((), ())), preferred_element_type=F32)
        return made.reshape(highs, GROUP, FIRST)

    def pair_of_groups(i, carry):
        both = jnp.concatenate([one_group(2 * i), one_group(2 * i + 1)], axis=1).astype(BF16)
        row = pl.multiple_of(i * 2 * GROUP, 2 * GROUP)
        for h in range(highs):
            dense_ref[pl.ds(row, 2 * GROUP), h * FIRST : (h + 1) * FIRST] = both[h]
        return carry

    lax.fori_loop(0, groups // 2, pair_of_groups, 0, unroll=UNROLL)


def build_dense(place, ids, weights, width, chunk):
    terms = ids.shape[0]
    queries = ids.shape[1] // CHUNKS
    groups = queries // GROUP
    rows = pltpu.VMEM((groups, GROUP * terms), F32)
    vmem = pl.BlockSpec(memory_space=pltpu.VMEM)
    return pl.pallas_call(
        functools.partial(dense_kernel, first=chunk * queries),
        out_shape=pltpu.VMEM((queries, width), BF16),
        in_specs=[pl.BlockSpec(memory_space=pltpu.SMEM), vmem, vmem],
        out_specs=vmem,
        scratch_shapes=[pltpu.VMEM((queries, LANES), F32), rows, rows, rows],
        compiler_params=pltpu.CompilerParams(vmem_limit_bytes=6 << 20),
        cost_estimate=pl.CostEstimate(flops=10**10, transcendentals=0, bytes_accessed=queries * width * 2),
        name="dense_build",
    )(place, ids, weights)


def rows_kernel(pos_ref, r0, r1, r2, r3, impact_ref, o0, o1, o2, o3):
    y = pos_ref[3]
    width = impact_ref.shape[0]
    full = r0.shape[0]
    rows = jnp.concatenate([r[:, :width] for r in (r0, r1, r2, r3)], axis=0)
    scores = jnp.dot(rows, impact_ref[...], preferred_element_type=F32)
    blocks = impact_ref.shape[1] // BLOCK
    for home, (r, o) in enumerate(((r0, o0), (r1, o1), (r2, o2), (r3, o3))):
        named = r[:, width : width + LANES].astype(F32).astype(jnp.int32) - y * blocks
        mine = scores[home * full : (home + 1) * full]
        for c in range(CANDS):
            column = named[:, c : c + 1]
            picked = jnp.zeros((full, BLOCK), F32)
            for b in range(blocks):
                picked = jnp.where(column == b, mine[:, b * BLOCK : (b + 1) * BLOCK], picked)
            o[c * full : (c + 1) * full, :] = picked.astype(BF16)


def score_rows(place, gathered, impact):
    full = gathered[0].shape[0]
    one = jax.ShapeDtypeStruct((full * CANDS, BLOCK), BF16)
    vmem = pl.BlockSpec(memory_space=pltpu.VMEM)
    return pl.pallas_call(
        rows_kernel,
        out_shape=[one] * NY,
        in_specs=[pl.BlockSpec(memory_space=pltpu.SMEM)] + [vmem] * 5,
        out_specs=[vmem] * NY,
        compiler_params=pltpu.CompilerParams(vmem_limit_bytes=8 << 20),
        cost_estimate=pl.CostEstimate(flops=2 * 10**9, transcendentals=0, bytes_accessed=4 << 20),
        name="score_rows",
    )(place, *gathered, impact)


def score_kernel(pos_ref, impact_ref, dense_ref, *refs, extra, steps):
    piece_refs = refs[:6]
    extra_refs = refs[6:10] if extra else ()
    out_refs = refs[-NZ - 3 : -3]
    made_ref, own_ref, own_sem = refs[-3:]
    x, z, core = pos_ref[0], pos_ref[1], pos_ref[2]
    depth, share = piece_refs[0].shape
    chunk = made_ref.shape[1]
    rows = chunk // steps
    half = LANES // 2
    copies = []
    for i in range(2):
        at = (pl.ds((core ^ i) * depth, depth), pl.ds(x * share, share))
        copies.append(pltpu.make_async_copy(impact_ref.at[at], own_ref.at[i], own_sem.at[i]))
        copies[i].start()
    left = lax.broadcasted_iota(jnp.int32, (rows, LANES), 1) < half
    for step in range(steps):
        made = [None, None]
        for i in (2, 3, 4, 5, 6, 7, 0, 1):
            if step == 0 and i == 0:
                for copy in copies:
                    copy.wait()
            piece = own_ref[i] if i < 2 else piece_refs[i - 2][...]
            for part in range(2):
                first = part * chunk + step * rows
                block = dense_ref[first : first + rows, i * depth : (i + 1) * depth]
                one = jnp.dot(block, piece, preferred_element_type=F32)
                made[part] = one if made[part] is None else made[part] + one
        for m in range(NZ // 2):
            a = made[0][:, m * LANES : (m + 1) * LANES]
            b = made[1][:, m * LANES : (m + 1) * LANES]
            at = slice(step * rows, (step + 1) * rows)
            made_ref[2 * m, at, :] = jnp.where(left, a, pltpu.roll(b, half, 1)).astype(BF16)
            made_ref[2 * m + 1, at, :] = jnp.where(left, pltpu.roll(a, half, 1), b).astype(BF16)
    for j, out_ref in enumerate(out_refs):
        out_ref[:chunk, :] = made_ref[(z + j) & (NZ - 1)]
    if extra:
        pack_rows(z, chunk, extra_refs, out_refs)


def pack_rows(z, chunk, extra_refs, out_refs):
    total = extra_refs[0][...].astype(F32)
    for r in extra_refs[1:]:
        total = total + r[...].astype(F32)
    wide, own = LANES // NX, LANES // (NX * NZ)
    deep = total.shape[0] // NZ
    place = (lax.broadcasted_iota(jnp.int32, (deep, LANES), 1) & (wide - 1)) // own
    for j, out_ref in enumerate(out_refs):
        to_z = (z + j) & (NZ - 1)
        packed = jnp.zeros((deep, LANES), F32)
        for g in range(NZ):
            part = total[g * deep : (g + 1) * deep]
            part = pltpu.roll(part, ((g - to_z) * own) & (LANES - 1), 1)
            packed = jnp.where(place == g, part, packed)
        out_ref[chunk:, :] = jnp.concatenate([packed, jnp.zeros_like(packed)], axis=0).astype(BF16)


def score_chunk(place, impact, dense, pieces, sums):
    chunk = dense.shape[0] // 2
    width = dense.shape[1]
    depth, share = pieces[0].shape
    extra = sums is not None
    out_rows = chunk + (2 * sums[0].shape[0] // NZ if extra else 0)
    more = tuple(sums) if extra else ()
    vmem = pl.BlockSpec(memory_space=pltpu.VMEM)
    hbm = pl.BlockSpec(memory_space=pltpu.HBM)
    return pl.pallas_call(
        functools.partial(score_kernel, extra=extra, steps=2),
        out_shape=[jax.ShapeDtypeStruct((out_rows, LANES), BF16)] * NZ,
        in_specs=[pl.BlockSpec(memory_space=pltpu.SMEM), hbm] + [vmem] * (1 + len(pieces) + len(more)),
        out_specs=[vmem] * NZ,
        scratch_shapes=[
            pltpu.VMEM((NZ, chunk, LANES), BF16),
            pltpu.VMEM((2, depth, share), BF16),
            pltpu.SemaphoreType.DMA((2,)),
        ],
        compiler_params=pltpu.CompilerParams(vmem_limit_bytes=12 << 20),
        cost_estimate=pl.CostEstimate(
            flops=2 * chunk * width * share * 2, transcendentals=0, bytes_accessed=chunk * width * 4
        ),
        name="score_chunk",
    )(place, kept_in_hbm(impact), dense, *pieces, *more)


def cut_kernel(pos_ref, impact_ref, query_ref, named_ref, ids_ref, weights_ref, *refs, shifts):
    rows_ref, ids_here, weights_here = refs[:3]
    out_refs, named_here, sem = refs[3:-2], refs[-2], refs[-1]
    x, core = pos_ref[0], pos_ref[2]
    full, width = query_ref.shape
    count = len(out_refs) * CUTS
    copies = [
        pltpu.make_async_copy(named_ref, named_here, sem.at[count]),
        pltpu.make_async_copy(query_ref, rows_ref.at[:, pl.ds(0, width)], sem.at[count + 1]),
        pltpu.make_async_copy(ids_ref, ids_here, sem.at[count + 2]),
        pltpu.make_async_copy(weights_ref, weights_here, sem.at[count + 3]),
    ]
    for i, (out_ref, r) in enumerate(zip(out_refs, shifts)):
        depth, share = out_ref.shape
        part = depth // CUTS
        to_x = (x - r) & (NX - 1)
        for j in range(CUTS):
            at = (pl.ds(core * depth + j * part, part), pl.ds(to_x * share, share))
            copies.append(
                pltpu.make_async_copy(impact_ref.at[at], out_ref.at[pl.ds(j * part, part)], sem.at[i * CUTS + j])
            )
    for copy in copies:
        copy.start()
    copies[0].wait()
    named = named_here[...].astype(F32)
    named = jnp.concatenate([named, jnp.zeros((LANES - CANDS, full), F32)], axis=0)
    rows_ref[:, width:] = named.T.astype(BF16)
    for copy in copies[1:]:
        copy.wait()


def cut_slices(place, impact, query_rows, candidates, ids, weights, shifts):
    full, width = query_rows.shape
    one = jax.ShapeDtypeStruct((impact.shape[0] // 2, impact.shape[1] // NX), BF16)
    vmem = pl.BlockSpec(memory_space=pltpu.VMEM)
    hbm = pl.BlockSpec(memory_space=pltpu.HBM)
    rows, ids_here, weights_here, *cuts = pl.pallas_call(
        functools.partial(cut_kernel, shifts=shifts),
        out_shape=[
            jax.ShapeDtypeStruct((full, width + LANES), BF16),
            jax.ShapeDtypeStruct(ids.shape, ids.dtype),
            jax.ShapeDtypeStruct(weights.shape, weights.dtype),
        ]
        + [one] * len(shifts),
        in_specs=[pl.BlockSpec(memory_space=pltpu.SMEM)] + [hbm] * 5,
        out_specs=[vmem] * (3 + len(shifts)),
        scratch_shapes=[
            pltpu.VMEM((CANDS, full), jnp.int32),
            pltpu.SemaphoreType.DMA((len(shifts) * CUTS + 4,)),
        ],
        compiler_params=pltpu.CompilerParams(vmem_limit_bytes=4 << 20),
        name="cut_slices",
    )(place, *[kept_in_hbm(a) for a in (impact, query_rows, candidates.T, ids, weights)])
    return rows, ids_here, weights_here, cuts


def summed_chunk(parts, to_ref, column):
    half = LANES // 2
    chunk = to_ref.shape[1] // 2 if column is None else to_ref.shape[1] // 4
    column = column or 0
    total = parts[0][:chunk].astype(F32)
    for part in parts[1:]:
        total = total + part[:chunk].astype(F32)
    turned = total.T.astype(BF16)
    to_ref[:, column : column + chunk] = turned[:half]
    to_ref[:, column + chunk : column + 2 * chunk] = turned[half:]


def half_kernel(a0, a1, a2, done_ref):
    summed_chunk((a0, a1, a2), done_ref, None)


def finish_half(parts, chunk):
    vmem = pl.BlockSpec(memory_space=pltpu.VMEM)
    return pl.pallas_call(
        half_kernel,
        out_shape=jax.ShapeDtypeStruct((LANES // 2, 2 * chunk), BF16),
        in_specs=[vmem] * 3,
        out_specs=vmem,
        compiler_params=pltpu.CompilerParams(vmem_limit_bytes=4 << 20),
        name="finish_half",
    )(*parts)


def final_kernel(pos_ref, done_ref, b0, b1, b2, v0, v1, v2, v3, first_ref, rescored_ref):
    x = pos_ref[0]
    columns = done_ref.shape[1]
    first_ref[:, :columns] = done_ref[...]
    summed_chunk((b0, b1, b2), first_ref, columns)
    more = v0[...].astype(F32) + v1[...].astype(F32) + v2[...].astype(F32) + v3[...].astype(F32)
    share = LANES // (NX * NZ)
    deep = more.shape[0] // 2
    turned = pltpu.roll(more, (LANES - x * (LANES // NX)) & (LANES - 1), 1).T
    for g in range(NZ):
        part = turned[g * share : (g + 1) * share, :deep]
        rescored_ref[g // 2, :, (g % 2) * deep : (g % 2 + 1) * deep] = part


def finish(place, done, parts, sums, full):
    vmem = pl.BlockSpec(memory_space=pltpu.VMEM)
    return pl.pallas_call(
        final_kernel,
        out_shape=[
            jax.ShapeDtypeStruct((LANES // 2, 2 * done.shape[1]), BF16),
            jax.ShapeDtypeStruct((CANDS, LANES // (NX * NZ), full), F32),
        ],
        in_specs=[pl.BlockSpec(memory_space=pltpu.SMEM)] + [vmem] * 8,
        out_specs=[vmem] * 2,
        compiler_params=pltpu.CompilerParams(vmem_limit_bytes=8 << 20),
        name="finish",
    )(place, done, *parts, *sums)


def added(*parts):
    total = parts[0].astype(F32)
    for part in parts[1:]:
        total = total + part.astype(F32)
    return total.astype(BF16)


def after(values, done):
    return lax.optimization_barrier((values, done))[0]


def sent(values):
    out = {}
    for way in (1, -1):
        out[way] = shifted(values[way], "z", way)
    return out


def first_step(made, long_way):
    ahead = shifted(made[4], "z", 2 * long_way)
    return ahead, sent({1: made[3], -1: made[5]})


def second_values(made, long_way, ahead, carried):
    values = {1: [carried[1], made[2]], -1: [carried[-1], made[6]]}
    values[long_way].append(ahead)
    return {way: added(*parts) for way, parts in values.items()}


def third_values(made, carried):
    return {1: added(carried[1], made[1]), -1: added(carried[-1], made[7])}


def rings(made_a, made_b, start_a, start_b):
    (ahead_a, going_a), (ahead_b, going_b) = start_a, start_b
    going_a = sent(second_values(made_a, 1, ahead_a, going_a))
    going_b = sent(second_values(made_b, -1, ahead_b, going_b))
    going_a = sent(third_values(made_a, going_a))
    going_b = sent(third_values(made_b, going_b))
    return (going_a[1], going_a[-1]), (going_b[1], going_b[-1])


def scored(term_ids, term_weights, impact, query_rows, candidates):
    x = lax.axis_index("x")
    z = lax.axis_index("z")
    y = lax.axis_index("prange")
    core = lax.axis_index("query")
    place = jnp.stack([x, z, core, y]).astype(jnp.int32)
    shard_width = impact.shape[0]
    full = query_rows.shape[0]

    shifts = (1, 3, 2)
    rows, ids, weights, cuts = cut_slices(place, impact, query_rows, candidates, term_ids.T, term_weights.T, shifts)
    near = {}
    for r, one in zip(shifts, cuts):
        near[r] = shifted(one, "x", -r)
    gathered = [rows]
    for r in (1, 2, 3):
        gathered.append(shifted(rows, "prange", -r))
    dense_a = build_dense(place, ids, weights, NX * shard_width, 0)
    gathered = after(gathered, dense_a)
    by_home = score_rows(place, gathered, impact)
    back = [by_home[0]]
    for r in (1, 2, 3):
        back.append(shifted(by_home[r], "prange", r))
    ids = after(ids, by_home)
    dense_b = build_dense(place, ids, weights, NX * shard_width, 1)

    pieces = {}
    for r in (1, 3, 2):
        ready = after(near[r], dense_b)
        pieces[r] = [ready, shifted(ready, "query", 1)]
    back = after(back, dense_b)
    pieces = pieces[1] + pieces[2] + pieces[3]
    made_a = score_chunk(place, impact, dense_a, pieces, back)
    start_a = first_step(made_a, 1)
    made_b = score_chunk(place, impact, dense_b, pieces, None)
    start_b = first_step(made_b, -1)
    (a1, a2), (b1, b2) = rings(made_a, made_b, start_a, start_b)
    chunk = made_b[0].shape[0]
    mine = added(made_a[0][chunk:], a1[chunk:], a2[chunk:])
    sums = [mine]
    for r in (1, 2, 3):
        sums.append(shifted(mine, "x", r))
    done = finish_half((made_a[0], a1, a2), chunk)
    first, rescored = finish(place, done, (made_b[0], b1, b2), sums, full)
    return (first[None], jnp.transpose(rescored, (2, 0, 1)))


def solution(mesh):
    finer = Mesh(
        mesh.devices.reshape(NX, NZ, mesh.shape["prange"], mesh.shape["query"]),
        ("x", "z", "prange", "query"),
    )
    vocab = ("x", "z")
    in_specs = (
        P("query", None),
        P("query", None),
        P(vocab, "prange"),
        P(("prange", "query"), vocab),
        P(("prange", "query"), None),
    )
    out_specs = (P("prange", vocab, "query"), P(("prange", "query"), None, vocab))
    return jax.shard_map(scored, mesh=finer, in_specs=in_specs, out_specs=out_specs, check_vma=False)
```

profile of v0, /device:TPU:2, one launch (start us, length us, event | category | flops | bytes accessed | tf_op | source)
XLA Modules:
  0.0 100.1 jit_solution(12140591447623847041)
XLA Ops:
  0.6 0.1 pad_add_fusion.pos_ref
  0.7 2.4 %cut_slices.1 = (bf16[16,1152]{1,0:T(8,128)(2,1)S(1)}, s32[32,2048]{1,0:T(8,128)S(1)}, bf16[32,2048]{1,0:T(8,128)(2,1)S(1)}, bf16[512,512]{1,0:T(8,128)(2,1)S(1)...) custom-call(s32[4]{0:T(128)S(1)} %pad_add_fusion.pos_ref, bf16[1024,2048]{1,0:T(8,128)(2,1)} %impact_ref.7, ...), custom_call_target="tpu_custom_call" | custom-call | tf_op jit(solution)/shard_map/cut_slices/pallas_call | solution.py:256
  3.2 1.7 %collective-permute-start.3 = (bf16[16,1152]{1,0:T(8,128)(2,1)S(1)}, bf16[16,1152]{1,0:T(8,128)(2,1)S(1)}, u32[]{:S(2)}, u32[]{:S(2)}) collective-permute-start(bf16[16,1152]{1,0:T(8,128)(2,1)S(1)} %get-tuple-element.46.r0), channel_id=1, source_target_pairs={{0,2},{2,4},{4,6},{6,0},{1,3},{3,5},{5,7},{7,1},{8,10},{10,12},{12... | collective-permute-start | bytes 110600 | tf_op jit(solution)/shard_map/ppermute | solution.py:29
  4.8 2.9 %collective-permute-start.2 = (bf16[16,1152]{1,0:T(8,128)(2,1)S(1)}, bf16[16,1152]{1,0:T(8,128)(2,1)S(1)}, u32[]{:S(2)}, u32[]{:S(2)}) collective-permute-start(bf16[16,1152]{1,0:T(8,128)(2,1)S(1)} %get-tuple-element.46.r0), channel_id=1, source_target_pairs={{0,4},{2,6},{4,0},{6,2},{1,5},{3,7},{5,1},{7,3},{8,12},{10,14},{12... | collective-permute-start | bytes 110600 | tf_op jit(solution)/shard_map/ppermute | solution.py:29
  7.7 1.3 %collective-permute-start.1 = (bf16[16,1152]{1,0:T(8,128)(2,1)S(1)}, bf16[16,1152]{1,0:T(8,128)(2,1)S(1)}, u32[]{:S(2)}, u32[]{:S(2)}) collective-permute-start(bf16[16,1152]{1,0:T(8,128)(2,1)S(1)} %get-tuple-element.46.r0), channel_id=1, source_target_pairs={{0,6},{2,0},{4,2},{6,4},{1,7},{3,1},{5,3},{7,5},{8,14},{10,8},{12,... | collective-permute-start | bytes 110600 | tf_op jit(solution)/shard_map/ppermute | solution.py:29
  9.1 0.5 collective-permute-start
  9.6 2.4 %collective-permute-start.5 = (bf16[512,512]{1,0:T(8,128)(2,1)S(1)}, bf16[512,512]{1,0:T(8,128)(2,1)S(1)}, u32[]{:S(2)}, u32[]{:S(2)}) collective-permute-start(bf16[512,512]{1,0:T(8,128)(2,1)S(1)} %get-tuple-element.56), channel_id=1, source_target_pairs={{0,128},{64,192},{128,0},{192,64},{1,129},{65,193},{129,1},{193,65... | collective-permute-start | bytes 1572872 | tf_op jit(solution)/shard_map/ppermute | solution.py:29
  12.0 6.9 %dense_build.2.dense_ref = bf16[1024,4096]{1,0:T(8,128)(2,1)S(1)} custom-call(s32[4]{0:T(128)S(1)} %pad_add_fusion.pos_ref, s32[32,2048]{1,0:T(8,128)S(1)} %get-tuple-element.54.ids_ref, bf16[32,2048]{1,0:T(8,128)(2,1)S(1)} %get-tuple-element.43.weights_ref), custom_call_target="tpu_custom_call" | custom-call | flops 10000000000 | bytes 8388608 | tf_op jit(solution)/shard_map/dense_build/pallas_call | solution.py:91
  19.0 0.0 collective-permute-done.3.r3
  19.0 1.9 %collective-permute-start.7 = (bf16[512,512]{1,0:T(8,128)(2,1)S(1)}, bf16[512,512]{1,0:T(8,128)(2,1)S(1)}, u32[]{:S(2)}, u32[]{:S(2)}) collective-permute-start(bf16[512,512]{1,0:T(8,128)(2,1)S(1)} %get-tuple-element.58), channel_id=1, source_target_pairs={{0,64},{64,128},{128,192},{192,0},{1,65},{65,129},{129,193},{193,1... | collective-permute-start | bytes 1572872 | tf_op jit(solution)/shard_map/ppermute | solution.py:29
  20.9 0.0 collective-permute-done.2.r2
  20.9 0.0 collective-permute-done.1.r1
  20.9 1.5 %score_rows.1 = (bf16[64,128]{1,0:T(8,128)(2,1)S(1)}, bf16[64,128]{1,0:T(8,128)(2,1)S(1)}, bf16[64,128]{1,0:T(8,128)(2,1)S(1)}, bf16[64,128]{1,0:T(8,128)(2,1)S(1)}) custom-call(s32[4]{0:T(128)S(1)} %pad_add_fusion.pos_ref, bf16[16,1152]{1,0:T(8,128)(2,1)S(1)} %get-tuple-element.46.r0, bf16[16,1152]{1,0:T(8,128)(2,1)S(1)} %collective-permute-done.1.r1, ...), custom_call_target="tpu_custom_call" | custom-call | flops 2000000000 | bytes 4194304 | tf_op jit(solution)/shard_map/score_rows/pallas_call | solution.py:125
  22.3 6.9 %dense_build.3.dense_ref = bf16[1024,4096]{1,0:T(8,128)(2,1)S(1)} custom-call(s32[4]{0:T(128)S(1)} %pad_add_fusion.pos_ref, s32[32,2048]{1,0:T(8,128)S(1)} %get-tuple-element.54.ids_ref, bf16[32,2048]{1,0:T(8,128)(2,1)S(1)} %get-tuple-element.43.weights_ref), custom_call_target="tpu_custom_call" | custom-call | flops 10000000000 | bytes 8388608 | tf_op jit(solution)/shard_map/dense_build/pallas_call | solution.py:91
  29.3 5.6 %collective-permute-done.7.refs_4_ = bf16[512,512]{1,0:T(8,128)(2,1)S(1)} collective-permute-done((bf16[512,512]{1,0:T(8,128)(2,1)S(1)}, bf16[512,512]{1,0:T(8,128)(2,1)S(1)}, u32[]{:S(2)}, u32[]{:S(2)}) %collective-permute-start.7) | collective-permute-done | bytes 524320 | tf_op jit(solution)/shard_map/ppermute | solution.py:29
  34.9 0.0 collective-permute-done.5.refs_2_
  34.9 0.0 collective-permute-done.refs_0_
  34.9 0.0 collective-permute-start.4
  34.9 0.5 collective-permute-start.6
  35.4 0.1 collective-permute-start.8
  35.5 0.7 collective-permute-start.9
  36.2 1.1 %collective-permute-start.10 = (bf16[64,128]{1,0:T(8,128)(2,1)S(1)}, bf16[64,128]{1,0:T(8,128)(2,1)S(1)}, u32[]{:S(2)}, u32[]{:S(2)}) collective-permute-start(bf16[64,128]{1,0:T(8,128)(2,1)S(1)} %get-tuple-element.52), channel_id=1, source_target_pairs={{0,4},{2,6},{4,0},{6,2},{1,5},{3,7},{5,1},{7,3},{8,12},{10,14},{12... | collective-permute-start | bytes 49160 | tf_op jit(solution)/shard_map/ppermute | solution.py:29
  37.3 3.2 %collective-permute-done.9.refs_7_ = bf16[64,128]{1,0:T(8,128)(2,1)S(1)} collective-permute-done((bf16[64,128]{1,0:T(8,128)(2,1)S(1)}, bf16[64,128]{1,0:T(8,128)(2,1)S(1)}, u32[]{:S(2)}, u32[]{:S(2)}) %collective-permute-start.9) | collective-permute-done | bytes 16416 | tf_op jit(solution)/shard_map/ppermute | solution.py:29
  40.5 0.0 collective-permute-start.11
  40.5 1.0 collective-permute-done.10.refs_8_
  41.4 2.8 %collective-permute-done.11.refs_9_ = bf16[64,128]{1,0:T(8,128)(2,1)S(1)} collective-permute-done((bf16[64,128]{1,0:T(8,128)(2,1)S(1)}, bf16[64,128]{1,0:T(8,128)(2,1)S(1)}, u32[]{:S(2)}, u32[]{:S(2)}) %collective-permute-start.11) | collective-permute-done | bytes 16416 | tf_op jit(solution)/shard_map/ppermute | solution.py:29
  44.2 0.0 collective-permute-done.4.refs_1_
  44.2 0.0 collective-permute-done.6.refs_3_
  44.2 0.0 collective-permute-done.8.refs_5_
  44.2 6.4 %score_chunk.3 = (bf16[512,128]{1,0:T(8,128)(2,1)S(1)}, bf16[512,128]{1,0:T(8,128)(2,1)S(1)}, bf16[512,128]{1,0:T(8,128)(2,1)S(1)}, bf16[512,128]{1,0:T(8,128)(2...) custom-call(s32[4]{0:T(128)S(1)} %pad_add_fusion.pos_ref, ...), custom_call_target="tpu_custom_call" | custom-call | flops 4294967296 | bytes 8388608 | tf_op jit(solution)/shard_map/score_chunk/pallas_call | solution.py:202
  50.7 2.0 %collective-permute-start.19 = (bf16[512,128]{1,0:T(8,128)(2,1)S(1)}, bf16[512,128]{1,0:T(8,128)(2,1)S(1)}, u32[]{:S(2)}, u32[]{:S(2)}) collective-permute-start(bf16[512,128]{1,0:T(8,128)(2,1)S(1)} %get-tuple-element.73), channel_id=1, source_target_pairs={{0,8},{8,16},{16,24},{24,32},{32,40},{40,48},{48,56},{56,0},{1,9},... | collective-permute-start | bytes 393224 | tf_op jit(solution)/shard_map/ppermute | solution.py:29
  52.7 4.0 %collective-permute-start.22 = (bf16[512,128]{1,0:T(8,128)(2,1)S(1)}, bf16[512,128]{1,0:T(8,128)(2,1)S(1)}, u32[]{:S(2)}, u32[]{:S(2)}) collective-permute-start(bf16[512,128]{1,0:T(8,128)(2,1)S(1)} %get-tuple-element.76), channel_id=1, source_target_pairs={{0,56},{8,0},{16,8},{24,16},{32,24},{40,32},{48,40},{56,48},{1,57}... | collective-permute-start | bytes 393224 | tf_op jit(solution)/shard_map/ppermute | solution.py:29
  56.7 2.4 %collective-permute-start.23 = (bf16[512,128]{1,0:T(8,128)(2,1)S(1)}, bf16[512,128]{1,0:T(8,128)(2,1)S(1)}, u32[]{:S(2)}, u32[]{:S(2)}) collective-permute-start(bf16[512,128]{1,0:T(8,128)(2,1)S(1)} %get-tuple-element.78), channel_id=1, source_target_pairs={{0,48},{8,56},{16,0},{24,8},{32,16},{40,24},{48,32},{56,40},{1,49}... | collective-permute-start | bytes 393224 | tf_op jit(solution)/shard_map/ppermute | solution.py:29
  59.1 6.4 %score_chunk.2 = (bf16[528,128]{1,0:T(8,128)(2,1)S(1)}, bf16[528,128]{1,0:T(8,128)(2,1)S(1)}, bf16[528,128]{1,0:T(8,128)(2,1)S(1)}, bf16[528,128]{1,0:T(8,128)(2...) custom-call(s32[4]{0:T(128)S(1)} %pad_add_fusion.pos_ref, ...), custom_call_target="tpu_custom_call" | custom-call | flops 4294967296 | bytes 8388608 | tf_op jit(solution)/shard_map/score_chunk/pallas_call | solution.py:202
  65.6 1.1 %collective-permute-start.12 = (bf16[528,128]{1,0:T(8,128)(2,1)S(1)}, bf16[528,128]{1,0:T(8,128)(2,1)S(1)}, u32[]{:S(2)}, u32[]{:S(2)}) collective-permute-start(bf16[528,128]{1,0:T(8,128)(2,1)S(1)} %get-tuple-element.65), channel_id=1, source_target_pairs={{0,8},{8,16},{16,24},{24,32},{32,40},{40,48},{48,56},{56,0},{1,9},... | collective-permute-start | bytes 405512 | tf_op jit(solution)/shard_map/ppermute | solution.py:29
  66.7 0.0 collective-permute-start.13
  66.7 0.0 collective-permute-done.19
  66.7 3.0 %collective-permute-start.16 = (bf16[528,128]{1,0:T(8,128)(2,1)S(1)}, bf16[528,128]{1,0:T(8,128)(2,1)S(1)}, u32[]{:S(2)}, u32[]{:S(2)}) collective-permute-start(bf16[528,128]{1,0:T(8,128)(2,1)S(1)} %get-tuple-element.69), channel_id=1, source_target_pairs={{0,56},{8,0},{16,8},{24,16},{32,24},{40,32},{48,40},{56,48},{1,57}... | collective-permute-start | bytes 405512 | tf_op jit(solution)/shard_map/ppermute | solution.py:29
  69.7 0.0 collective-permute-done.22
  69.7 0.1 collective-permute-start.20
  69.8 0.0 collective-permute-done.23
  69.8 0.1 add_convert_fusion.5
  69.9 3.3 %collective-permute-start.24 = (bf16[512,128]{1,0:T(8,128)(2,1)S(1)}, bf16[512,128]{1,0:T(8,128)(2,1)S(1)}, u32[]{:S(2)}, u32[]{:S(2)}) collective-permute-start(bf16[512,128]{1,0:T(8,128)(2,1)S(1)} %add_convert_fusion.5), channel_id=1, source_target_pairs={{0,56},{8,0},{16,8},{24,16},{32,24},{40,32},{48,40},{56,48},{1,57}... | collective-permute-start | bytes 393224 | tf_op jit(solution)/shard_map/ppermute | solution.py:29
  73.1 0.2 collective-permute-done.12
  73.3 3.9 %collective-permute-done.13 = bf16[528,128]{1,0:T(8,128)(2,1)S(1)} collective-permute-done((bf16[528,128]{1,0:T(8,128)(2,1)S(1)}, bf16[528,128]{1,0:T(8,128)(2,1)S(1)}, u32[]{:S(2)}, u32[]{:S(2)}) %collective-permute-start.13) | collective-permute-done | bytes 135200 | tf_op jit(solution)/shard_map/ppermute | solution.py:29
  77.3 0.1 add_convert_fusion.3
  77.3 2.0 %collective-permute-start.14 = (bf16[528,128]{1,0:T(8,128)(2,1)S(1)}, bf16[528,128]{1,0:T(8,128)(2,1)S(1)}, u32[]{:S(2)}, u32[]{:S(2)}) collective-permute-start(bf16[528,128]{1,0:T(8,128)(2,1)S(1)} %add_convert_fusion.3), channel_id=1, source_target_pairs={{0,8},{8,16},{16,24},{24,32},{32,40},{40,48},{48,56},{56,0},{1,9},... | collective-permute-start | bytes 405512 | tf_op jit(solution)/shard_map/ppermute | solution.py:29
  79.3 1.4 %collective-permute-start.17 = (bf16[528,128]{1,0:T(8,128)(2,1)S(1)}, bf16[528,128]{1,0:T(8,128)(2,1)S(1)}, u32[]{:S(2)}, u32[]{:S(2)}) collective-permute-start(bf16[528,128]{1,0:T(8,128)(2,1)S(1)} %add_convert_fusion.1), channel_id=1, source_target_pairs={{0,56},{8,0},{16,8},{24,16},{32,24},{40,32},{48,40},{56,48},{1,57}... | collective-permute-start | bytes 405512 | tf_op jit(solution)/shard_map/ppermute | solution.py:29
  80.8 0.7 collective-permute-start.21
  81.5 2.8 %collective-permute-done.14 = bf16[528,128]{1,0:T(8,128)(2,1)S(1)} collective-permute-done((bf16[528,128]{1,0:T(8,128)(2,1)S(1)}, bf16[528,128]{1,0:T(8,128)(2,1)S(1)}, u32[]{:S(2)}, u32[]{:S(2)}) %collective-permute-start.14) | collective-permute-done | bytes 135200 | tf_op jit(solution)/shard_map/ppermute | solution.py:29
  84.4 0.9 collective-permute-start.15
  85.3 0.2 collective-permute-done.17
  85.5 2.6 %collective-permute-start.18 = (bf16[528,128]{1,0:T(8,128)(2,1)S(1)}, bf16[528,128]{1,0:T(8,128)(2,1)S(1)}, u32[]{:S(2)}, u32[]{:S(2)}) collective-permute-start(bf16[528,128]{1,0:T(8,128)(2,1)S(1)} %add_convert_fusion), channel_id=1, source_target_pairs={{0,56},{8,0},{16,8},{24,16},{32,24},{40,32},{48,40},{56,48},{1,57}... | collective-permute-start | bytes 405512 | tf_op jit(solution)/shard_map/ppermute | solution.py:29
  88.1 0.0 collective-permute-done.24
  88.1 0.1 collective-permute-start.25
  88.2 2.4 %collective-permute-done.15.a1 = bf16[528,128]{1,0:T(8,128)(2,1)S(1)} collective-permute-done((bf16[528,128]{1,0:T(8,128)(2,1)S(1)}, bf16[528,128]{1,0:T(8,128)(2,1)S(1)}, u32[]{:S(2)}, u32[]{:S(2)}) %collective-permute-start.15) | collective-permute-done | bytes 135200 | tf_op jit(solution)/shard_map/ppermute | solution.py:29
  90.7 2.8 %collective-permute-start.28 = (bf16[16,128]{1,0:T(8,128)(2,1)S(1)}, bf16[16,128]{1,0:T(8,128)(2,1)S(1)}, u32[]{:S(2)}, u32[]{:S(2)}) collective-permute-start(bf16[16,128]{1,0:T(8,128)(2,1)S(1)} %add_convert_fusion.8.v0), channel_id=1, source_target_pairs={{0,192},{64,0},{128,64},{192,128},{1,193},{65,1},{129,65},{193,129... | collective-permute-start | bytes 12296 | tf_op jit(solution)/shard_map/ppermute | solution.py:29
  93.5 0.2 collective-permute-start.27
  93.8 1.8 %collective-permute-start.26 = (bf16[16,128]{1,0:T(8,128)(2,1)S(1)}, bf16[16,128]{1,0:T(8,128)(2,1)S(1)}, u32[]{:S(2)}, u32[]{:S(2)}) collective-permute-start(bf16[16,128]{1,0:T(8,128)(2,1)S(1)} %add_convert_fusion.8.v0), channel_id=1, source_target_pairs={{0,64},{64,128},{128,192},{192,0},{1,65},{65,129},{129,193},{193,1... | collective-permute-start | bytes 12296 | tf_op jit(solution)/shard_map/ppermute | solution.py:29
  95.6 0.1 finish_half.1.done_ref
  95.7 0.0 collective-permute-done.25.b2
  95.7 0.0 collective-permute-done.28.v3
  95.8 2.9 %collective-permute-done.27.v2 = bf16[16,128]{1,0:T(8,128)(2,1)S(1)} collective-permute-done((bf16[16,128]{1,0:T(8,128)(2,1)S(1)}, bf16[16,128]{1,0:T(8,128)(2,1)S(1)}, u32[]{:S(2)}, u32[]{:S(2)}) %collective-permute-start.27) | collective-permute-done | bytes 4128 | tf_op jit(solution)/shard_map/ppermute | solution.py:29
  98.6 1.4 %finish.1 = (bf16[64,2048]{1,0:T(8,128)(2,1)}, f32[4,4,16]{2,1,0:T(4,128)}) custom-call(s32[4]{0:T(128)S(1)} %pad_add_fusion.pos_ref, bf16[64,1024]{1,0:T(8,128)(2,1)S(1)} %finish_half.1.done_ref, bf16[512,128]{1,0:T(8,128)(2,1)S(1)} %get-tuple-element.72.b0, bf16[512,128]{1,0:T(8,128)(2,1)S(1)} %collective-permute-done.21.b1, ...), custom_call_target="tpu_custom_call" | custom-call | tf_op jit(solution)/shard_map/finish/pallas_call | solution.py:320
  (14 shorter events, 0.3 us)
Async XLA Ops:
  3.2 15.8 %collective-permute-start.3 = (bf16[16,1152]{1,0:T(8,128)(2,1)S(1)}, bf16[16,1152]{1,0:T(8,128)(2,1)S(1)}, u32[]{:S(2)}, u32[]{:S(2)}) collective-permute-start(bf16[16,1152]{1,0:T(8,128)(2,1)S(1)} %get-tuple-element.46.r0), channel_id=1, source_target_pairs={{0,2},{2,4},{4,6},{6,0},{1,3},{3,5},{5,7},{7,1},{8,10},{10,12},{12... | collective-permute-start | bytes 110600 | tf_op jit(solution)/shard_map/ppermute | solution.py:29
  4.8 16.0 %collective-permute-start.2 = (bf16[16,1152]{1,0:T(8,128)(2,1)S(1)}, bf16[16,1152]{1,0:T(8,128)(2,1)S(1)}, u32[]{:S(2)}, u32[]{:S(2)}) collective-permute-start(bf16[16,1152]{1,0:T(8,128)(2,1)S(1)} %get-tuple-element.46.r0), channel_id=1, source_target_pairs={{0,4},{2,6},{4,0},{6,2},{1,5},{3,7},{5,1},{7,3},{8,12},{10,14},{12... | collective-permute-start | bytes 110600 | tf_op jit(solution)/shard_map/ppermute | solution.py:29
  7.7 13.1 %collective-permute-start.1 = (bf16[16,1152]{1,0:T(8,128)(2,1)S(1)}, bf16[16,1152]{1,0:T(8,128)(2,1)S(1)}, u32[]{:S(2)}, u32[]{:S(2)}) collective-permute-start(bf16[16,1152]{1,0:T(8,128)(2,1)S(1)} %get-tuple-element.46.r0), channel_id=1, source_target_pairs={{0,6},{2,0},{4,2},{6,4},{1,7},{3,1},{5,3},{7,5},{8,14},{10,8},{12,... | collective-permute-start | bytes 110600 | tf_op jit(solution)/shard_map/ppermute | solution.py:29
  9.1 25.9 %collective-permute-start = (bf16[512,512]{1,0:T(8,128)(2,1)S(1)}, bf16[512,512]{1,0:T(8,128)(2,1)S(1)}, u32[]{:S(2)}, u32[]{:S(2)}) collective-permute-start(bf16[512,512]{1,0:T(8,128)(2,1)S(1)} %get-tuple-element.44), channel_id=1, source_target_pairs={{0,192},{64,0},{128,64},{192,128},{1,193},{65,1},{129,65},{193,129... | collective-permute-start | bytes 1572872 | tf_op jit(solution)/shard_map/ppermute | solution.py:29
  9.6 25.3 %collective-permute-start.5 = (bf16[512,512]{1,0:T(8,128)(2,1)S(1)}, bf16[512,512]{1,0:T(8,128)(2,1)S(1)}, u32[]{:S(2)}, u32[]{:S(2)}) collective-permute-start(bf16[512,512]{1,0:T(8,128)(2,1)S(1)} %get-tuple-element.56), channel_id=1, source_target_pairs={{0,128},{64,192},{128,0},{192,64},{1,129},{65,193},{129,1},{193,65... | collective-permute-start | bytes 1572872 | tf_op jit(solution)/shard_map/ppermute | solution.py:29
  12.0 8.8 %copy-start = (bf16[1024,2048]{1,0:T(8,128)(2,1)S(1)}, bf16[1024,2048]{1,0:T(8,128)(2,1)}, u32[]{:S(2)}) copy-start(bf16[1024,2048]{1,0:T(8,128)(2,1)} %impact_ref.7) | copy-start | bytes 12582916
  19.0 15.9 %collective-permute-start.7 = (bf16[512,512]{1,0:T(8,128)(2,1)S(1)}, bf16[512,512]{1,0:T(8,128)(2,1)S(1)}, u32[]{:S(2)}, u32[]{:S(2)}) collective-permute-start(bf16[512,512]{1,0:T(8,128)(2,1)S(1)} %get-tuple-element.58), channel_id=1, source_target_pairs={{0,64},{64,128},{128,192},{192,0},{1,65},{65,129},{129,193},{193,1... | collective-permute-start | bytes 1572872 | tf_op jit(solution)/shard_map/ppermute | solution.py:29
  34.9 9.3 %collective-permute-start.4 = (bf16[512,512]{1,0:T(8,128)(2,1)S(1)}, bf16[512,512]{1,0:T(8,128)(2,1)S(1)}, u32[]{:S(2)}, u32[]{:S(2)}) collective-permute-start(bf16[512,512]{1,0:T(8,128)(2,1)S(1)} %collective-permute-done.refs_0_), channel_id=1, source_target_pairs={{0,1},{1,0},{2,3},{3,2},{4,5},{5,4},{6,7},{7,6},{8,9},{9,8},{10,11... | collective-permute-start | bytes 1572872 | tf_op jit(solution)/shard_map/ppermute | solution.py:29
  34.9 9.3 %collective-permute-start.6 = (bf16[512,512]{1,0:T(8,128)(2,1)S(1)}, bf16[512,512]{1,0:T(8,128)(2,1)S(1)}, u32[]{:S(2)}, u32[]{:S(2)}) collective-permute-start(bf16[512,512]{1,0:T(8,128)(2,1)S(1)} %collective-permute-done.5.refs_2_), channel_id=1, source_target_pairs={{0,1},{1,0},{2,3},{3,2},{4,5},{5,4},{6,7},{7,6},{8,9},{9,8},{10,11... | collective-permute-start | bytes 1572872 | tf_op jit(solution)/shard_map/ppermute | solution.py:29
  35.4 8.8 %collective-permute-start.8 = (bf16[512,512]{1,0:T(8,128)(2,1)S(1)}, bf16[512,512]{1,0:T(8,128)(2,1)S(1)}, u32[]{:S(2)}, u32[]{:S(2)}) collective-permute-start(bf16[512,512]{1,0:T(8,128)(2,1)S(1)} %collective-permute-done.7.refs_4_), channel_id=1, source_target_pairs={{0,1},{1,0},{2,3},{3,2},{4,5},{5,4},{6,7},{7,6},{8,9},{9,8},{10,11... | collective-permute-start | bytes 1572872 | tf_op jit(solution)/shard_map/ppermute | solution.py:29
  35.5 5.0 %collective-permute-start.9 = (bf16[64,128]{1,0:T(8,128)(2,1)S(1)}, bf16[64,128]{1,0:T(8,128)(2,1)S(1)}, u32[]{:S(2)}, u32[]{:S(2)}) collective-permute-start(bf16[64,128]{1,0:T(8,128)(2,1)S(1)} %get-tuple-element.51), channel_id=1, source_target_pairs={{0,2},{2,4},{4,6},{6,0},{1,3},{3,5},{5,7},{7,1},{8,10},{10,12},{12... | collective-permute-start | bytes 49160 | tf_op jit(solution)/shard_map/ppermute | solution.py:29
  36.2 5.2 %collective-permute-start.10 = (bf16[64,128]{1,0:T(8,128)(2,1)S(1)}, bf16[64,128]{1,0:T(8,128)(2,1)S(1)}, u32[]{:S(2)}, u32[]{:S(2)}) collective-permute-start(bf16[64,128]{1,0:T(8,128)(2,1)S(1)} %get-tuple-element.52), channel_id=1, source_target_pairs={{0,4},{2,6},{4,0},{6,2},{1,5},{3,7},{5,1},{7,3},{8,12},{10,14},{12... | collective-permute-start | bytes 49160 | tf_op jit(solution)/shard_map/ppermute | solution.py:29
  40.5 3.7 %collective-permute-start.11 = (bf16[64,128]{1,0:T(8,128)(2,1)S(1)}, bf16[64,128]{1,0:T(8,128)(2,1)S(1)}, u32[]{:S(2)}, u32[]{:S(2)}) collective-permute-start(bf16[64,128]{1,0:T(8,128)(2,1)S(1)} %get-tuple-element.53), channel_id=1, source_target_pairs={{0,6},{2,0},{4,2},{6,4},{1,7},{3,1},{5,3},{7,5},{8,14},{10,8},{12,... | collective-permute-start | bytes 49160 | tf_op jit(solution)/shard_map/ppermute | solution.py:29
  50.7 16.0 %collective-permute-start.19 = (bf16[512,128]{1,0:T(8,128)(2,1)S(1)}, bf16[512,128]{1,0:T(8,128)(2,1)S(1)}, u32[]{:S(2)}, u32[]{:S(2)}) collective-permute-start(bf16[512,128]{1,0:T(8,128)(2,1)S(1)} %get-tuple-element.73), channel_id=1, source_target_pairs={{0,8},{8,16},{16,24},{24,32},{32,40},{40,48},{48,56},{56,0},{1,9},... | collective-permute-start | bytes 393224 | tf_op jit(solution)/shard_map/ppermute | solution.py:29
  52.7 17.0 %collective-permute-start.22 = (bf16[512,128]{1,0:T(8,128)(2,1)S(1)}, bf16[512,128]{1,0:T(8,128)(2,1)S(1)}, u32[]{:S(2)}, u32[]{:S(2)}) collective-permute-start(bf16[512,128]{1,0:T(8,128)(2,1)S(1)} %get-tuple-element.76), channel_id=1, source_target_pairs={{0,56},{8,0},{16,8},{24,16},{32,24},{40,32},{48,40},{56,48},{1,57}... | collective-permute-start | bytes 393224 | tf_op jit(solution)/shard_map/ppermute | solution.py:29
  56.7 13.1 %collective-permute-start.23 = (bf16[512,128]{1,0:T(8,128)(2,1)S(1)}, bf16[512,128]{1,0:T(8,128)(2,1)S(1)}, u32[]{:S(2)}, u32[]{:S(2)}) collective-permute-start(bf16[512,128]{1,0:T(8,128)(2,1)S(1)} %get-tuple-element.78), channel_id=1, source_target_pairs={{0,48},{8,56},{16,0},{24,8},{32,16},{40,24},{48,32},{56,40},{1,49}... | collective-permute-start | bytes 393224 | tf_op jit(solution)/shard_map/ppermute | solution.py:29
  65.6 7.7 %collective-permute-start.12 = (bf16[528,128]{1,0:T(8,128)(2,1)S(1)}, bf16[528,128]{1,0:T(8,128)(2,1)S(1)}, u32[]{:S(2)}, u32[]{:S(2)}) collective-permute-start(bf16[528,128]{1,0:T(8,128)(2,1)S(1)} %get-tuple-element.65), channel_id=1, source_target_pairs={{0,8},{8,16},{16,24},{24,32},{32,40},{40,48},{48,56},{56,0},{1,9},... | collective-permute-start | bytes 405512 | tf_op jit(solution)/shard_map/ppermute | solution.py:29
  66.7 10.6 %collective-permute-start.13 = (bf16[528,128]{1,0:T(8,128)(2,1)S(1)}, bf16[528,128]{1,0:T(8,128)(2,1)S(1)}, u32[]{:S(2)}, u32[]{:S(2)}) collective-permute-start(bf16[528,128]{1,0:T(8,128)(2,1)S(1)} %get-tuple-element.67), channel_id=1, source_target_pairs={{0,16},{8,24},{16,32},{24,40},{32,48},{40,56},{48,0},{56,8},{1,17}... | collective-permute-start | bytes 405512 | tf_op jit(solution)/shard_map/ppermute | solution.py:29
  66.7 12.6 %collective-permute-start.16 = (bf16[528,128]{1,0:T(8,128)(2,1)S(1)}, bf16[528,128]{1,0:T(8,128)(2,1)S(1)}, u32[]{:S(2)}, u32[]{:S(2)}) collective-permute-start(bf16[528,128]{1,0:T(8,128)(2,1)S(1)} %get-tuple-element.69), channel_id=1, source_target_pairs={{0,56},{8,0},{16,8},{24,16},{32,24},{40,32},{48,40},{56,48},{1,57}... | collective-permute-start | bytes 405512 | tf_op jit(solution)/shard_map/ppermute | solution.py:29
  69.7 11.1 %collective-permute-start.20 = (bf16[512,128]{1,0:T(8,128)(2,1)S(1)}, bf16[512,128]{1,0:T(8,128)(2,1)S(1)}, u32[]{:S(2)}, u32[]{:S(2)}) collective-permute-start(bf16[512,128]{1,0:T(8,128)(2,1)S(1)} %add_convert_fusion.7), channel_id=1, source_target_pairs={{0,8},{8,16},{16,24},{24,32},{32,40},{40,48},{48,56},{56,0},{1,9},... | collective-permute-start | bytes 393224 | tf_op jit(solution)/shard_map/ppermute | solution.py:29
  69.9 18.2 %collective-permute-start.24 = (bf16[512,128]{1,0:T(8,128)(2,1)S(1)}, bf16[512,128]{1,0:T(8,128)(2,1)S(1)}, u32[]{:S(2)}, u32[]{:S(2)}) collective-permute-start(bf16[512,128]{1,0:T(8,128)(2,1)S(1)} %add_convert_fusion.5), channel_id=1, source_target_pairs={{0,56},{8,0},{16,8},{24,16},{32,24},{40,32},{48,40},{56,48},{1,57}... | collective-permute-start | bytes 393224 | tf_op jit(solution)/shard_map/ppermute | solution.py:29
  77.3 7.0 %collective-permute-start.14 = (bf16[528,128]{1,0:T(8,128)(2,1)S(1)}, bf16[528,128]{1,0:T(8,128)(2,1)S(1)}, u32[]{:S(2)}, u32[]{:S(2)}) collective-permute-start(bf16[528,128]{1,0:T(8,128)(2,1)S(1)} %add_convert_fusion.3), channel_id=1, source_target_pairs={{0,8},{8,16},{16,24},{24,32},{32,40},{40,48},{48,56},{56,0},{1,9},... | collective-permute-start | bytes 405512 | tf_op jit(solution)/shard_map/ppermute | solution.py:29
  79.3 6.2 %collective-permute-start.17 = (bf16[528,128]{1,0:T(8,128)(2,1)S(1)}, bf16[528,128]{1,0:T(8,128)(2,1)S(1)}, u32[]{:S(2)}, u32[]{:S(2)}) collective-permute-start(bf16[528,128]{1,0:T(8,128)(2,1)S(1)} %add_convert_fusion.1), channel_id=1, source_target_pairs={{0,56},{8,0},{16,8},{24,16},{32,24},{40,32},{48,40},{56,48},{1,57}... | collective-permute-start | bytes 405512 | tf_op jit(solution)/shard_map/ppermute | solution.py:29
  80.8 14.9 %collective-permute-start.21 = (bf16[512,128]{1,0:T(8,128)(2,1)S(1)}, bf16[512,128]{1,0:T(8,128)(2,1)S(1)}, u32[]{:S(2)}, u32[]{:S(2)}) collective-permute-start(bf16[512,128]{1,0:T(8,128)(2,1)S(1)} %add_convert_fusion.6), channel_id=1, source_target_pairs={{0,8},{8,16},{16,24},{24,32},{32,40},{40,48},{48,56},{56,0},{1,9},... | collective-permute-start | bytes 393224 | tf_op jit(solution)/shard_map/ppermute | solution.py:29
  84.4 6.3 %collective-permute-start.15 = (bf16[528,128]{1,0:T(8,128)(2,1)S(1)}, bf16[528,128]{1,0:T(8,128)(2,1)S(1)}, u32[]{:S(2)}, u32[]{:S(2)}) collective-permute-start(bf16[528,128]{1,0:T(8,128)(2,1)S(1)} %add_convert_fusion.2), channel_id=1, source_target_pairs={{0,8},{8,16},{16,24},{24,32},{32,40},{40,48},{48,56},{56,0},{1,9},... | collective-permute-start | bytes 405512 | tf_op jit(solution)/shard_map/ppermute | solution.py:29
  85.5 5.2 %collective-permute-start.18 = (bf16[528,128]{1,0:T(8,128)(2,1)S(1)}, bf16[528,128]{1,0:T(8,128)(2,1)S(1)}, u32[]{:S(2)}, u32[]{:S(2)}) collective-permute-start(bf16[528,128]{1,0:T(8,128)(2,1)S(1)} %add_convert_fusion), channel_id=1, source_target_pairs={{0,56},{8,0},{16,8},{24,16},{32,24},{40,32},{48,40},{56,48},{1,57}... | collective-permute-start | bytes 405512 | tf_op jit(solution)/shard_map/ppermute | solution.py:29
  88.1 7.6 %collective-permute-start.25 = (bf16[512,128]{1,0:T(8,128)(2,1)S(1)}, bf16[512,128]{1,0:T(8,128)(2,1)S(1)}, u32[]{:S(2)}, u32[]{:S(2)}) collective-permute-start(bf16[512,128]{1,0:T(8,128)(2,1)S(1)} %add_convert_fusion.4), channel_id=1, source_target_pairs={{0,56},{8,0},{16,8},{24,16},{32,24},{40,32},{48,40},{56,48},{1,57}... | collective-permute-start | bytes 393224 | tf_op jit(solution)/shard_map/ppermute | solution.py:29
  90.7 5.1 %collective-permute-start.28 = (bf16[16,128]{1,0:T(8,128)(2,1)S(1)}, bf16[16,128]{1,0:T(8,128)(2,1)S(1)}, u32[]{:S(2)}, u32[]{:S(2)}) collective-permute-start(bf16[16,128]{1,0:T(8,128)(2,1)S(1)} %add_convert_fusion.8.v0), channel_id=1, source_target_pairs={{0,192},{64,0},{128,64},{192,128},{1,193},{65,1},{129,65},{193,129... | collective-permute-start | bytes 12296 | tf_op jit(solution)/shard_map/ppermute | solution.py:29
  93.5 5.1 %collective-permute-start.27 = (bf16[16,128]{1,0:T(8,128)(2,1)S(1)}, bf16[16,128]{1,0:T(8,128)(2,1)S(1)}, u32[]{:S(2)}, u32[]{:S(2)}) collective-permute-start(bf16[16,128]{1,0:T(8,128)(2,1)S(1)} %add_convert_fusion.8.v0), channel_id=1, source_target_pairs={{0,128},{64,192},{128,0},{192,64},{1,129},{65,193},{129,1},{193,65... | collective-permute-start | bytes 12296 | tf_op jit(solution)/shard_map/ppermute | solution.py:29
  93.8 4.9 %collective-permute-start.26 = (bf16[16,128]{1,0:T(8,128)(2,1)S(1)}, bf16[16,128]{1,0:T(8,128)(2,1)S(1)}, u32[]{:S(2)}, u32[]{:S(2)}) collective-permute-start(bf16[16,128]{1,0:T(8,128)(2,1)S(1)} %add_convert_fusion.8.v0), channel_id=1, source_target_pairs={{0,64},{64,128},{128,192},{192,0},{1,65},{65,129},{129,193},{193,1... | collective-permute-start | bytes 12296 | tf_op jit(solution)/shard_map/ppermute | solution.py:29
where the time goes:
time: 100 us
  starting transfers between devices  41.6 us (42%)
  Pallas kernels  32.2 us (32%)
  waiting for transfers between devices  25 us (25%)
    ppermute x29, starting transfers between devices, shifted(): lax.ppermute(array, axis, [(i, (i + shift) % size) for i in range(size)])  41.6 us
    ppermute x29, waiting for transfers between devices, shifted(): lax.ppermute(array, axis, [(i, (i + shift) % size) for i in range(size)])  25 us
    pallas_call x2, Pallas kernels, build_dense(): pl.pallas_call(functools.partial(dense_kernel, first=chunk * queries), ou...  13.9 us
    pallas_call x2, Pallas kernels, score_chunk(): pl.pallas_call(functools.partial(score_kernel, extra=extra, steps=2), out...  12.9 us
    pallas_call x1, Pallas kernels, cut_slices(): pl.pallas_call(functools.partial(cut_kernel, shifts=shifts), out_shape=[j...  2.44 us
  transfers between devices with their start and end apart: 29, of which 10 were waited for; matrix products, arithmetic and copies ran while one was open for 0% of the time, Pallas kernels for 22%

commit v1 on v0

--- a/solution.py
+++ b/solution.py
@@ -200,7 +200,7 @@
     vmem = pl.BlockSpec(memory_space=pltpu.VMEM)
     hbm = pl.BlockSpec(memory_space=pltpu.HBM)
     return pl.pallas_call(
-        functools.partial(score_kernel, extra=extra, steps=2),
+        functools.partial(score_kernel, extra=extra, steps=1),
         out_shape=[jax.ShapeDtypeStruct((out_rows, LANES), BF16)] * NZ,
         in_specs=[pl.BlockSpec(memory_space=pltpu.SMEM), hbm] + [vmem] * (1 + len(pieces) + len(more)),
         out_specs=[vmem] * NZ,
@@ -289,7 +289,8 @@
     summed_chunk((a0, a1, a2), done_ref, None)
 
 
-def finish_half(parts, chunk):
+def finish_half(parts):
+    chunk = parts[0].shape[0]
     vmem = pl.BlockSpec(memory_space=pltpu.VMEM)
     return pl.pallas_call(
         half_kernel,
@@ -301,12 +302,13 @@
     )(*parts)
 
 
-def final_kernel(pos_ref, done_ref, b0, b1, b2, v0, v1, v2, v3, first_ref, rescored_ref):
+def final_kernel(pos_ref, done_ref, b0, b1, b2, first_ref, rescored_ref):
     x = pos_ref[0]
     columns = done_ref.shape[1]
     first_ref[:, :columns] = done_ref[...]
     summed_chunk((b0, b1, b2), first_ref, columns)
-    more = v0[...].astype(F32) + v1[...].astype(F32) + v2[...].astype(F32) + v3[...].astype(F32)
+    chunk = columns // 2
+    more = b0[chunk:].astype(F32) + b1[chunk:].astype(F32) + b2[chunk:].astype(F32)
     share = LANES // (NX * NZ)
     deep = more.shape[0] // 2
     turned = pltpu.roll(more, (LANES - x * (LANES // NX)) & (LANES - 1), 1).T
@@ -315,7 +317,7 @@
         rescored_ref[g // 2, :, (g % 2) * deep : (g % 2 + 1) * deep] = part
 
 
-def finish(place, done, parts, sums, full):
+def finish(place, done, parts, full):
     vmem = pl.BlockSpec(memory_space=pltpu.VMEM)
     return pl.pallas_call(
         final_kernel,
@@ -323,11 +325,11 @@
             jax.ShapeDtypeStruct((LANES // 2, 2 * done.shape[1]), BF16),
             jax.ShapeDtypeStruct((CANDS, LANES // (NX * NZ), full), F32),
         ],
-        in_specs=[pl.BlockSpec(memory_space=pltpu.SMEM)] + [vmem] * 8,
+        in_specs=[pl.BlockSpec(memory_space=pltpu.SMEM)] + [vmem] * 4,
         out_specs=[vmem] * 2,
         compiler_params=pltpu.CompilerParams(vmem_limit_bytes=8 << 20),
         name="finish",
-    )(place, done, *parts, *sums)
+    )(place, done, *parts)
 
 
 def added(*parts):
@@ -402,20 +404,18 @@
     for r in (1, 3, 2):
         ready = after(near[r], dense_b)
         pieces[r] = [ready, shifted(ready, "query", 1)]
-    back = after(back, dense_b)
-    pieces = pieces[1] + pieces[2] + pieces[3]
-    made_a = score_chunk(place, impact, dense_a, pieces, back)
-    start_a = first_step(made_a, 1)
-    made_b = score_chunk(place, impact, dense_b, pieces, None)
-    start_b = first_step(made_b, -1)
-    (a1, a2), (b1, b2) = rings(made_a, made_b, start_a, start_b)
-    chunk = made_b[0].shape[0]
-    mine = added(made_a[0][chunk:], a1[chunk:], a2[chunk:])
+    mine = added(*after(back, dense_b))
     sums = [mine]
     for r in (1, 2, 3):
         sums.append(shifted(mine, "x", r))
-    done = finish_half((made_a[0], a1, a2), chunk)
-    first, rescored = finish(place, done, (made_b[0], b1, b2), sums, full)
+    pieces = pieces[1] + pieces[2] + pieces[3]
+    made_a = score_chunk(place, impact, dense_a, pieces, None)
+    start_a = first_step(made_a, 1)
+    made_b = score_chunk(place, impact, dense_b, pieces, sums)
+    start_b = first_step(made_b, -1)
+    (a1, a2), (b1, b2) = rings(made_a, made_b, start_a, start_b)
+    done = finish_half((made_a[0], a1, a2))
+    first, rescored = finish(place, done, (made_b[0], b1, b2), full)
     return (first[None], jnp.transpose(rescored, (2, 0, 1)))
 
 

time: 100 us -> 97.4 us (0.974)
  starting transfers between devices: 41.6 us -> 40 us
  waiting for transfers between devices: 25 us -> 23.4 us
    ppermute x29, waiting for transfers between devices: 25 us -> 23.4 us  [shifted(): lax.ppermute(array, axis, [(i, (i + shift) % size) for i in range(size)])]
    ppermute x29, starting transfers between devices: 41.6 us -> 40 us  [shifted(): lax.ppermute(array, axis, [(i, (i + shift) % size) for i in range(size)])]
  transfers between devices with their start and end apart: 29 -> 29, of which waited for: 10 -> 9; matrix products, arithmetic and copies ran while one was open for 0% -> 0% of each run, Pallas kernels for 22% -> 29%
where the time goes in v1:
time: 97.4 us; the launch traced here: 96.7 us
  starting transfers between devices  40 us (41%)
  Pallas kernels  32.1 us (33%)
  waiting for transfers between devices  23.4 us (24%)
    ppermute x29, starting transfers between devices, shifted(): lax.ppermute(array, axis, [(i, (i + shift) % size) for i in range(size)])  40 us
    ppermute x29, waiting for transfers between devices, shifted(): lax.ppermute(array, axis, [(i, (i + shift) % size) for i in range(size)])  23.4 us
    pallas_call x2, Pallas kernels, build_dense(): pl.pallas_call(functools.partial(dense_kernel, first=chunk * queries), ou...  13.9 us
    pallas_call x2, Pallas kernels, score_chunk(): pl.pallas_call(functools.partial(score_kernel, extra=extra, steps=1), out...  12.8 us
    pallas_call x1, Pallas kernels, cut_slices(): pl.pallas_call(functools.partial(cut_kernel, shifts=shifts), out_shape=[j...  2.44 us
  transfers between devices with their start and end apart: 29, of which 9 were waited for; matrix products, arithmetic and copies ran while one was open for 0% of the time, Pallas kernels for 29%

profile of v1, /device:TPU:2, one launch (start us, length us, event | category | flops | bytes accessed | tf_op | source)
XLA Modules:
  0.0 96.7 jit_solution(17208620870744690666)
XLA Ops:
  0.6 0.1 pad_add_fusion.pos_ref
  0.7 2.4 %cut_slices.1 = (bf16[16,1152]{1,0:T(8,128)(2,1)S(1)}, s32[32,2048]{1,0:T(8,128)S(1)}, bf16[32,2048]{1,0:T(8,128)(2,1)S(1)}, bf16[512,512]{1,0:T(8,128)(2,1)S(1)...) custom-call(s32[4]{0:T(128)S(1)} %pad_add_fusion.pos_ref, bf16[1024,2048]{1,0:T(8,128)(2,1)} %impact_ref.7, ...), custom_call_target="tpu_custom_call" | custom-call | tf_op jit(solution)/shard_map/cut_slices/pallas_call | solution.py:256
  3.2 3.1 %collective-permute-start.1 = (bf16[16,1152]{1,0:T(8,128)(2,1)S(1)}, bf16[16,1152]{1,0:T(8,128)(2,1)S(1)}, u32[]{:S(2)}, u32[]{:S(2)}) collective-permute-start(bf16[16,1152]{1,0:T(8,128)(2,1)S(1)} %get-tuple-element.46.r0), channel_id=1, source_target_pairs={{0,6},{2,0},{4,2},{6,4},{1,7},{3,1},{5,3},{7,5},{8,14},{10,8},{12,... | collective-permute-start | bytes 110600 | tf_op jit(solution)/shard_map/ppermute | solution.py:29
  6.3 0.6 collective-permute-start.2
  6.9 1.0 %collective-permute-start.3 = (bf16[16,1152]{1,0:T(8,128)(2,1)S(1)}, bf16[16,1152]{1,0:T(8,128)(2,1)S(1)}, u32[]{:S(2)}, u32[]{:S(2)}) collective-permute-start(bf16[16,1152]{1,0:T(8,128)(2,1)S(1)} %get-tuple-element.46.r0), channel_id=1, source_target_pairs={{0,2},{2,4},{4,6},{6,0},{1,3},{3,5},{5,7},{7,1},{8,10},{10,12},{12... | collective-permute-start | bytes 110600 | tf_op jit(solution)/shard_map/ppermute | solution.py:29
  7.9 0.5 collective-permute-start
  8.4 2.4 %collective-permute-start.5 = (bf16[512,512]{1,0:T(8,128)(2,1)S(1)}, bf16[512,512]{1,0:T(8,128)(2,1)S(1)}, u32[]{:S(2)}, u32[]{:S(2)}) collective-permute-start(bf16[512,512]{1,0:T(8,128)(2,1)S(1)} %get-tuple-element.56), channel_id=1, source_target_pairs={{0,128},{64,192},{128,0},{192,64},{1,129},{65,193},{129,1},{193,65... | collective-permute-start | bytes 1572872 | tf_op jit(solution)/shard_map/ppermute | solution.py:29
  10.8 6.9 %dense_build.2.dense_ref = bf16[1024,4096]{1,0:T(8,128)(2,1)S(1)} custom-call(s32[4]{0:T(128)S(1)} %pad_add_fusion.pos_ref, s32[32,2048]{1,0:T(8,128)S(1)} %get-tuple-element.54.ids_ref, bf16[32,2048]{1,0:T(8,128)(2,1)S(1)} %get-tuple-element.43.weights_ref), custom_call_target="tpu_custom_call" | custom-call | flops 10000000000 | bytes 8388608 | tf_op jit(solution)/shard_map/dense_build/pallas_call | solution.py:91
  17.8 0.0 collective-permute-done.1.r1
  17.8 1.9 %collective-permute-start.7 = (bf16[512,512]{1,0:T(8,128)(2,1)S(1)}, bf16[512,512]{1,0:T(8,128)(2,1)S(1)}, u32[]{:S(2)}, u32[]{:S(2)}) collective-permute-start(bf16[512,512]{1,0:T(8,128)(2,1)S(1)} %get-tuple-element.58), channel_id=1, source_target_pairs={{0,64},{64,128},{128,192},{192,0},{1,65},{65,129},{129,193},{193,1... | collective-permute-start | bytes 1572872 | tf_op jit(solution)/shard_map/ppermute | solution.py:29
  19.6 0.0 collective-permute-done.2.r2
  19.6 0.0 collective-permute-done.3.r3
  19.7 1.5 %score_rows.1 = (bf16[64,128]{1,0:T(8,128)(2,1)S(1)}, bf16[64,128]{1,0:T(8,128)(2,1)S(1)}, bf16[64,128]{1,0:T(8,128)(2,1)S(1)}, bf16[64,128]{1,0:T(8,128)(2,1)S(1)}) custom-call(s32[4]{0:T(128)S(1)} %pad_add_fusion.pos_ref, bf16[16,1152]{1,0:T(8,128)(2,1)S(1)} %get-tuple-element.46.r0, bf16[16,1152]{1,0:T(8,128)(2,1)S(1)} %collective-permute-done.1.r1, ...), custom_call_target="tpu_custom_call" | custom-call | flops 2000000000 | bytes 4194304 | tf_op jit(solution)/shard_map/score_rows/pallas_call | solution.py:125
  21.1 6.9 %dense_build.3.dense_ref = bf16[1024,4096]{1,0:T(8,128)(2,1)S(1)} custom-call(s32[4]{0:T(128)S(1)} %pad_add_fusion.pos_ref, s32[32,2048]{1,0:T(8,128)S(1)} %get-tuple-element.54.ids_ref, bf16[32,2048]{1,0:T(8,128)(2,1)S(1)} %get-tuple-element.43.weights_ref), custom_call_target="tpu_custom_call" | custom-call | flops 10000000000 | bytes 8388608 | tf_op jit(solution)/shard_map/dense_build/pallas_call | solution.py:91
  28.1 0.0 collective-permute-done.refs_0_
  28.1 0.1 collective-permute-start.4
  28.2 4.6 %collective-permute-done.5.refs_2_ = bf16[512,512]{1,0:T(8,128)(2,1)S(1)} collective-permute-done((bf16[512,512]{1,0:T(8,128)(2,1)S(1)}, bf16[512,512]{1,0:T(8,128)(2,1)S(1)}, u32[]{:S(2)}, u32[]{:S(2)}) %collective-permute-start.5) | collective-permute-done | bytes 524320 | tf_op jit(solution)/shard_map/ppermute | solution.py:29
  32.8 0.0 collective-permute-start.6
  32.8 0.9 collective-permute-done.7.refs_4_
  33.7 0.0 collective-permute-start.8
  33.7 1.9 %collective-permute-start.16 = (bf16[64,128]{1,0:T(8,128)(2,1)S(1)}, bf16[64,128]{1,0:T(8,128)(2,1)S(1)}, u32[]{:S(2)}, u32[]{:S(2)}) collective-permute-start(bf16[64,128]{1,0:T(8,128)(2,1)S(1)} %get-tuple-element.51), channel_id=1, source_target_pairs={{0,2},{2,4},{4,6},{6,0},{1,3},{3,5},{5,7},{7,1},{8,10},{10,12},{12... | collective-permute-start | bytes 49160 | tf_op jit(solution)/shard_map/ppermute | solution.py:29
  35.6 1.8 %collective-permute-start.17 = (bf16[64,128]{1,0:T(8,128)(2,1)S(1)}, bf16[64,128]{1,0:T(8,128)(2,1)S(1)}, u32[]{:S(2)}, u32[]{:S(2)}) collective-permute-start(bf16[64,128]{1,0:T(8,128)(2,1)S(1)} %get-tuple-element.52), channel_id=1, source_target_pairs={{0,4},{2,6},{4,0},{6,2},{1,5},{3,7},{5,1},{7,3},{8,12},{10,14},{12... | collective-permute-start | bytes 49160 | tf_op jit(solution)/shard_map/ppermute | solution.py:29
  37.4 1.2 %collective-permute-done.16 = bf16[64,128]{1,0:T(8,128)(2,1)S(1)} collective-permute-done((bf16[64,128]{1,0:T(8,128)(2,1)S(1)}, bf16[64,128]{1,0:T(8,128)(2,1)S(1)}, u32[]{:S(2)}, u32[]{:S(2)}) %collective-permute-start.16) | collective-permute-done | bytes 16416 | tf_op jit(solution)/shard_map/ppermute | solution.py:29
  38.7 1.1 %collective-permute-start.18 = (bf16[64,128]{1,0:T(8,128)(2,1)S(1)}, bf16[64,128]{1,0:T(8,128)(2,1)S(1)}, u32[]{:S(2)}, u32[]{:S(2)}) collective-permute-start(bf16[64,128]{1,0:T(8,128)(2,1)S(1)} %get-tuple-element.53), channel_id=1, source_target_pairs={{0,6},{2,0},{4,2},{6,4},{1,7},{3,1},{5,3},{7,5},{8,14},{10,8},{12,... | collective-permute-start | bytes 49160 | tf_op jit(solution)/shard_map/ppermute | solution.py:29
  39.7 1.1 %collective-permute-done.17 = bf16[64,128]{1,0:T(8,128)(2,1)S(1)} collective-permute-done((bf16[64,128]{1,0:T(8,128)(2,1)S(1)}, bf16[64,128]{1,0:T(8,128)(2,1)S(1)}, u32[]{:S(2)}, u32[]{:S(2)}) %collective-permute-start.17) | collective-permute-done | bytes 16416 | tf_op jit(solution)/shard_map/ppermute | solution.py:29
  40.8 1.6 %collective-permute-done.18 = bf16[64,128]{1,0:T(8,128)(2,1)S(1)} collective-permute-done((bf16[64,128]{1,0:T(8,128)(2,1)S(1)}, bf16[64,128]{1,0:T(8,128)(2,1)S(1)}, u32[]{:S(2)}, u32[]{:S(2)}) %collective-permute-start.18) | collective-permute-done | bytes 16416 | tf_op jit(solution)/shard_map/ppermute | solution.py:29
  42.4 1.5 %collective-permute-start.19 = (bf16[64,128]{1,0:T(8,128)(2,1)S(1)}, bf16[64,128]{1,0:T(8,128)(2,1)S(1)}, u32[]{:S(2)}, u32[]{:S(2)}) collective-permute-start(bf16[64,128]{1,0:T(8,128)(2,1)S(1)} %add_convert_fusion.8.refs_6_), channel_id=1, source_target_pairs={{0,64},{64,128},{128,192},{192,0},{1,65},{65,129},{129,193},{193,1... | collective-permute-start | bytes 49160 | tf_op jit(solution)/shard_map/ppermute | solution.py:29
  44.0 3.3 %collective-permute-start.20 = (bf16[64,128]{1,0:T(8,128)(2,1)S(1)}, bf16[64,128]{1,0:T(8,128)(2,1)S(1)}, u32[]{:S(2)}, u32[]{:S(2)}) collective-permute-start(bf16[64,128]{1,0:T(8,128)(2,1)S(1)} %add_convert_fusion.8.refs_6_), channel_id=1, source_target_pairs={{0,128},{64,192},{128,0},{192,64},{1,129},{65,193},{129,1},{193,65... | collective-permute-start | bytes 49160 | tf_op jit(solution)/shard_map/ppermute | solution.py:29
  47.3 0.2 collective-permute-start.21
  47.5 0.0 collective-permute-done.6.refs_3_
  47.5 0.0 collective-permute-done.8.refs_5_
  47.5 6.4 %score_chunk.2 = (bf16[512,128]{1,0:T(8,128)(2,1)S(1)}, bf16[512,128]{1,0:T(8,128)(2,1)S(1)}, bf16[512,128]{1,0:T(8,128)(2,1)S(1)}, bf16[512,128]{1,0:T(8,128)(2...) custom-call(s32[4]{0:T(128)S(1)} %pad_add_fusion.pos_ref, ...), custom_call_target="tpu_custom_call" | custom-call | flops 4294967296 | bytes 8388608 | tf_op jit(solution)/shard_map/score_chunk/pallas_call | solution.py:202
  53.9 3.4 %collective-permute-start.10 = (bf16[512,128]{1,0:T(8,128)(2,1)S(1)}, bf16[512,128]{1,0:T(8,128)(2,1)S(1)}, u32[]{:S(2)}, u32[]{:S(2)}) collective-permute-start(bf16[512,128]{1,0:T(8,128)(2,1)S(1)} %get-tuple-element.63), channel_id=1, source_target_pairs={{0,16},{8,24},{16,32},{24,40},{32,48},{40,56},{48,0},{56,8},{1,17}... | collective-permute-start | bytes 393224 | tf_op jit(solution)/shard_map/ppermute | solution.py:29
  57.2 1.9 %collective-permute-start.9 = (bf16[512,128]{1,0:T(8,128)(2,1)S(1)}, bf16[512,128]{1,0:T(8,128)(2,1)S(1)}, u32[]{:S(2)}, u32[]{:S(2)}) collective-permute-start(bf16[512,128]{1,0:T(8,128)(2,1)S(1)} %get-tuple-element.61), channel_id=1, source_target_pairs={{0,8},{8,16},{16,24},{24,32},{32,40},{40,48},{48,56},{56,0},{1,9},... | collective-permute-start | bytes 393224 | tf_op jit(solution)/shard_map/ppermute | solution.py:29
  59.1 0.0 collective-permute-done.19.refs_7_
  59.1 1.3 %collective-permute-start.13 = (bf16[512,128]{1,0:T(8,128)(2,1)S(1)}, bf16[512,128]{1,0:T(8,128)(2,1)S(1)}, u32[]{:S(2)}, u32[]{:S(2)}) collective-permute-start(bf16[512,128]{1,0:T(8,128)(2,1)S(1)} %get-tuple-element.65), channel_id=1, source_target_pairs={{0,56},{8,0},{16,8},{24,16},{32,24},{40,32},{48,40},{56,48},{1,57}... | collective-permute-start | bytes 393224 | tf_op jit(solution)/shard_map/ppermute | solution.py:29
  60.4 0.0 collective-permute-done.20.refs_8_
  60.5 0.0 collective-permute-done.21.refs_9_
  60.5 6.4 %score_chunk.3 = (bf16[528,128]{1,0:T(8,128)(2,1)S(1)}, bf16[528,128]{1,0:T(8,128)(2,1)S(1)}, bf16[528,128]{1,0:T(8,128)(2,1)S(1)}, bf16[528,128]{1,0:T(8,128)(2...) custom-call(s32[4]{0:T(128)S(1)} %pad_add_fusion.pos_ref, ...), custom_call_target="tpu_custom_call" | custom-call | flops 4294967296 | bytes 8388608 | tf_op jit(solution)/shard_map/score_chunk/pallas_call | solution.py:202
  66.9 2.1 %collective-permute-start.22 = (bf16[528,128]{1,0:T(8,128)(2,1)S(1)}, bf16[528,128]{1,0:T(8,128)(2,1)S(1)}, u32[]{:S(2)}, u32[]{:S(2)}) collective-permute-start(bf16[528,128]{1,0:T(8,128)(2,1)S(1)} %get-tuple-element.73), channel_id=1, source_target_pairs={{0,8},{8,16},{16,24},{24,32},{32,40},{40,48},{48,56},{56,0},{1,9},... | collective-permute-start | bytes 405512 | tf_op jit(solution)/shard_map/ppermute | solution.py:29
  69.0 1.1 %collective-permute-start.26 = (bf16[528,128]{1,0:T(8,128)(2,1)S(1)}, bf16[528,128]{1,0:T(8,128)(2,1)S(1)}, u32[]{:S(2)}, u32[]{:S(2)}) collective-permute-start(bf16[528,128]{1,0:T(8,128)(2,1)S(1)} %get-tuple-element.78), channel_id=1, source_target_pairs={{0,48},{8,56},{16,0},{24,8},{32,16},{40,24},{48,32},{56,40},{1,49}... | collective-permute-start | bytes 405512 | tf_op jit(solution)/shard_map/ppermute | solution.py:29
  70.1 0.0 collective-permute-done.10
  70.1 1.5 %collective-permute-start.25 = (bf16[528,128]{1,0:T(8,128)(2,1)S(1)}, bf16[528,128]{1,0:T(8,128)(2,1)S(1)}, u32[]{:S(2)}, u32[]{:S(2)}) collective-permute-start(bf16[528,128]{1,0:T(8,128)(2,1)S(1)} %get-tuple-element.76), channel_id=1, source_target_pairs={{0,56},{8,0},{16,8},{24,16},{32,24},{40,32},{48,40},{56,48},{1,57}... | collective-permute-start | bytes 405512 | tf_op jit(solution)/shard_map/ppermute | solution.py:29
  71.6 0.0 collective-permute-done.9
  71.6 0.1 add_convert_fusion.7
  71.6 0.6 collective-permute-start.11
  72.3 0.0 collective-permute-done.13
  72.3 2.8 %collective-permute-start.14 = (bf16[512,128]{1,0:T(8,128)(2,1)S(1)}, bf16[512,128]{1,0:T(8,128)(2,1)S(1)}, u32[]{:S(2)}, u32[]{:S(2)}) collective-permute-start(bf16[512,128]{1,0:T(8,128)(2,1)S(1)} %add_convert_fusion.5), channel_id=1, source_target_pairs={{0,56},{8,0},{16,8},{24,16},{32,24},{40,32},{48,40},{56,48},{1,57}... | collective-permute-start | bytes 393224 | tf_op jit(solution)/shard_map/ppermute | solution.py:29
  75.1 0.0 collective-permute-done.22
  75.1 0.1 collective-permute-start.23
  75.2 2.2 %collective-permute-done.26 = bf16[528,128]{1,0:T(8,128)(2,1)S(1)} collective-permute-done((bf16[528,128]{1,0:T(8,128)(2,1)S(1)}, bf16[528,128]{1,0:T(8,128)(2,1)S(1)}, u32[]{:S(2)}, u32[]{:S(2)}) %collective-permute-start.26) | collective-permute-done | bytes 135200 | tf_op jit(solution)/shard_map/ppermute | solution.py:29
  77.4 3.2 %collective-permute-done.25 = bf16[528,128]{1,0:T(8,128)(2,1)S(1)} collective-permute-done((bf16[528,128]{1,0:T(8,128)(2,1)S(1)}, bf16[528,128]{1,0:T(8,128)(2,1)S(1)}, u32[]{:S(2)}, u32[]{:S(2)}) %collective-permute-start.25) | collective-permute-done | bytes 135200 | tf_op jit(solution)/shard_map/ppermute | solution.py:29
  80.6 0.1 add_convert_fusion.1
  80.7 1.5 %collective-permute-start.27 = (bf16[528,128]{1,0:T(8,128)(2,1)S(1)}, bf16[528,128]{1,0:T(8,128)(2,1)S(1)}, u32[]{:S(2)}, u32[]{:S(2)}) collective-permute-start(bf16[528,128]{1,0:T(8,128)(2,1)S(1)} %add_convert_fusion.1), channel_id=1, source_target_pairs={{0,56},{8,0},{16,8},{24,16},{32,24},{40,32},{48,40},{56,48},{1,57}... | collective-permute-start | bytes 405512 | tf_op jit(solution)/shard_map/ppermute | solution.py:29
  82.3 0.6 collective-permute-start.12
  83.0 0.7 collective-permute-start.24
  83.7 3.5 %collective-permute-done.27 = bf16[528,128]{1,0:T(8,128)(2,1)S(1)} collective-permute-done((bf16[528,128]{1,0:T(8,128)(2,1)S(1)}, bf16[528,128]{1,0:T(8,128)(2,1)S(1)}, u32[]{:S(2)}, u32[]{:S(2)}) %collective-permute-start.27) | collective-permute-done | bytes 135200 | tf_op jit(solution)/shard_map/ppermute | solution.py:29
  87.3 2.8 %collective-permute-start.28 = (bf16[528,128]{1,0:T(8,128)(2,1)S(1)}, bf16[528,128]{1,0:T(8,128)(2,1)S(1)}, u32[]{:S(2)}, u32[]{:S(2)}) collective-permute-start(bf16[528,128]{1,0:T(8,128)(2,1)S(1)} %add_convert_fusion), channel_id=1, source_target_pairs={{0,56},{8,0},{16,8},{24,16},{32,24},{40,32},{48,40},{56,48},{1,57}... | collective-permute-start | bytes 405512 | tf_op jit(solution)/shard_map/ppermute | solution.py:29
  90.0 0.0 collective-permute-done.14
  90.1 0.1 collective-permute-start.15
  90.2 4.9 %collective-permute-done.15.a2 = bf16[512,128]{1,0:T(8,128)(2,1)S(1)} collective-permute-done((bf16[512,128]{1,0:T(8,128)(2,1)S(1)}, bf16[512,128]{1,0:T(8,128)(2,1)S(1)}, u32[]{:S(2)}, u32[]{:S(2)}) %collective-permute-start.15) | collective-permute-done | bytes 131104 | tf_op jit(solution)/shard_map/ppermute | solution.py:29
  95.1 0.1 finish_half.1.done_ref
  95.3 0.0 collective-permute-done.28.b2
  95.3 1.4 %finish.1 = (bf16[64,2048]{1,0:T(8,128)(2,1)}, f32[4,4,16]{2,1,0:T(4,128)}) custom-call(s32[4]{0:T(128)S(1)} %pad_add_fusion.pos_ref, bf16[64,1024]{1,0:T(8,128)(2,1)S(1)} %finish_half.1.done_ref, bf16[528,128]{1,0:T(8,128)(2,1)S(1)} %get-tuple-element.72.b0, bf16[528,128]{1,0:T(8,128)(2,1)S(1)} %collective-permute-done.24.b1, ...), custom_call_target="tpu_custom_call" | custom-call | tf_op jit(solution)/shard_map/finish/pallas_call | solution.py:322
  (14 shorter events, 0.3 us)
Async XLA Ops:
  3.2 14.6 %collective-permute-start.1 = (bf16[16,1152]{1,0:T(8,128)(2,1)S(1)}, bf16[16,1152]{1,0:T(8,128)(2,1)S(1)}, u32[]{:S(2)}, u32[]{:S(2)}) collective-permute-start(bf16[16,1152]{1,0:T(8,128)(2,1)S(1)} %get-tuple-element.46.r0), channel_id=1, source_target_pairs={{0,6},{2,0},{4,2},{6,4},{1,7},{3,1},{5,3},{7,5},{8,14},{10,8},{12,... | collective-permute-start | bytes 110600 | tf_op jit(solution)/shard_map/ppermute | solution.py:29
  6.3 13.4 %collective-permute-start.2 = (bf16[16,1152]{1,0:T(8,128)(2,1)S(1)}, bf16[16,1152]{1,0:T(8,128)(2,1)S(1)}, u32[]{:S(2)}, u32[]{:S(2)}) collective-permute-start(bf16[16,1152]{1,0:T(8,128)(2,1)S(1)} %get-tuple-element.46.r0), channel_id=1, source_target_pairs={{0,4},{2,6},{4,0},{6,2},{1,5},{3,7},{5,1},{7,3},{8,12},{10,14},{12... | collective-permute-start | bytes 110600 | tf_op jit(solution)/shard_map/ppermute | solution.py:29
  6.9 12.8 %collective-permute-start.3 = (bf16[16,1152]{1,0:T(8,128)(2,1)S(1)}, bf16[16,1152]{1,0:T(8,128)(2,1)S(1)}, u32[]{:S(2)}, u32[]{:S(2)}) collective-permute-start(bf16[16,1152]{1,0:T(8,128)(2,1)S(1)} %get-tuple-element.46.r0), channel_id=1, source_target_pairs={{0,2},{2,4},{4,6},{6,0},{1,3},{3,5},{5,7},{7,1},{8,10},{10,12},{12... | collective-permute-start | bytes 110600 | tf_op jit(solution)/shard_map/ppermute | solution.py:29
  7.9 20.2 %collective-permute-start = (bf16[512,512]{1,0:T(8,128)(2,1)S(1)}, bf16[512,512]{1,0:T(8,128)(2,1)S(1)}, u32[]{:S(2)}, u32[]{:S(2)}) collective-permute-start(bf16[512,512]{1,0:T(8,128)(2,1)S(1)} %get-tuple-element.44), channel_id=1, source_target_pairs={{0,192},{64,0},{128,64},{192,128},{1,193},{65,1},{129,65},{193,129... | collective-permute-start | bytes 1572872 | tf_op jit(solution)/shard_map/ppermute | solution.py:29
  8.4 24.5 %collective-permute-start.5 = (bf16[512,512]{1,0:T(8,128)(2,1)S(1)}, bf16[512,512]{1,0:T(8,128)(2,1)S(1)}, u32[]{:S(2)}, u32[]{:S(2)}) collective-permute-start(bf16[512,512]{1,0:T(8,128)(2,1)S(1)} %get-tuple-element.56), channel_id=1, source_target_pairs={{0,128},{64,192},{128,0},{192,64},{1,129},{65,193},{129,1},{193,65... | collective-permute-start | bytes 1572872 | tf_op jit(solution)/shard_map/ppermute | solution.py:29
  10.8 8.8 %copy-start = (bf16[1024,2048]{1,0:T(8,128)(2,1)S(1)}, bf16[1024,2048]{1,0:T(8,128)(2,1)}, u32[]{:S(2)}) copy-start(bf16[1024,2048]{1,0:T(8,128)(2,1)} %impact_ref.7) | copy-start | bytes 12582916
  17.8 15.9 %collective-permute-start.7 = (bf16[512,512]{1,0:T(8,128)(2,1)S(1)}, bf16[512,512]{1,0:T(8,128)(2,1)S(1)}, u32[]{:S(2)}, u32[]{:S(2)}) collective-permute-start(bf16[512,512]{1,0:T(8,128)(2,1)S(1)} %get-tuple-element.58), channel_id=1, source_target_pairs={{0,64},{64,128},{128,192},{192,0},{1,65},{65,129},{129,193},{193,1... | collective-permute-start | bytes 1572872 | tf_op jit(solution)/shard_map/ppermute | solution.py:29
  28.1 19.2 %collective-permute-start.4 = (bf16[512,512]{1,0:T(8,128)(2,1)S(1)}, bf16[512,512]{1,0:T(8,128)(2,1)S(1)}, u32[]{:S(2)}, u32[]{:S(2)}) collective-permute-start(bf16[512,512]{1,0:T(8,128)(2,1)S(1)} %collective-permute-done.refs_0_), channel_id=1, source_target_pairs={{0,1},{1,0},{2,3},{3,2},{4,5},{5,4},{6,7},{7,6},{8,9},{9,8},{10,11... | collective-permute-start | bytes 1572872 | tf_op jit(solution)/shard_map/ppermute | solution.py:29
  32.8 14.6 %collective-permute-start.6 = (bf16[512,512]{1,0:T(8,128)(2,1)S(1)}, bf16[512,512]{1,0:T(8,128)(2,1)S(1)}, u32[]{:S(2)}, u32[]{:S(2)}) collective-permute-start(bf16[512,512]{1,0:T(8,128)(2,1)S(1)} %collective-permute-done.5.refs_2_), channel_id=1, source_target_pairs={{0,1},{1,0},{2,3},{3,2},{4,5},{5,4},{6,7},{7,6},{8,9},{9,8},{10,11... | collective-permute-start | bytes 1572872 | tf_op jit(solution)/shard_map/ppermute | solution.py:29
  33.7 13.8 %collective-permute-start.8 = (bf16[512,512]{1,0:T(8,128)(2,1)S(1)}, bf16[512,512]{1,0:T(8,128)(2,1)S(1)}, u32[]{:S(2)}, u32[]{:S(2)}) collective-permute-start(bf16[512,512]{1,0:T(8,128)(2,1)S(1)} %collective-permute-done.7.refs_4_), channel_id=1, source_target_pairs={{0,1},{1,0},{2,3},{3,2},{4,5},{5,4},{6,7},{7,6},{8,9},{9,8},{10,11... | collective-permute-start | bytes 1572872 | tf_op jit(solution)/shard_map/ppermute | solution.py:29
  33.7 5.0 %collective-permute-start.16 = (bf16[64,128]{1,0:T(8,128)(2,1)S(1)}, bf16[64,128]{1,0:T(8,128)(2,1)S(1)}, u32[]{:S(2)}, u32[]{:S(2)}) collective-permute-start(bf16[64,128]{1,0:T(8,128)(2,1)S(1)} %get-tuple-element.51), channel_id=1, source_target_pairs={{0,2},{2,4},{4,6},{6,0},{1,3},{3,5},{5,7},{7,1},{8,10},{10,12},{12... | collective-permute-start | bytes 49160 | tf_op jit(solution)/shard_map/ppermute | solution.py:29
  35.6 5.2 %collective-permute-start.17 = (bf16[64,128]{1,0:T(8,128)(2,1)S(1)}, bf16[64,128]{1,0:T(8,128)(2,1)S(1)}, u32[]{:S(2)}, u32[]{:S(2)}) collective-permute-start(bf16[64,128]{1,0:T(8,128)(2,1)S(1)} %get-tuple-element.52), channel_id=1, source_target_pairs={{0,4},{2,6},{4,0},{6,2},{1,5},{3,7},{5,1},{7,3},{8,12},{10,14},{12... | collective-permute-start | bytes 49160 | tf_op jit(solution)/shard_map/ppermute | solution.py:29
  38.7 3.7 %collective-permute-start.18 = (bf16[64,128]{1,0:T(8,128)(2,1)S(1)}, bf16[64,128]{1,0:T(8,128)(2,1)S(1)}, u32[]{:S(2)}, u32[]{:S(2)}) collective-permute-start(bf16[64,128]{1,0:T(8,128)(2,1)S(1)} %get-tuple-element.53), channel_id=1, source_target_pairs={{0,6},{2,0},{4,2},{6,4},{1,7},{3,1},{5,3},{7,5},{8,14},{10,8},{12,... | collective-permute-start | bytes 49160 | tf_op jit(solution)/shard_map/ppermute | solution.py:29
  42.4 16.7 %collective-permute-start.19 = (bf16[64,128]{1,0:T(8,128)(2,1)S(1)}, bf16[64,128]{1,0:T(8,128)(2,1)S(1)}, u32[]{:S(2)}, u32[]{:S(2)}) collective-permute-start(bf16[64,128]{1,0:T(8,128)(2,1)S(1)} %add_convert_fusion.8.refs_6_), channel_id=1, source_target_pairs={{0,64},{64,128},{128,192},{192,0},{1,65},{65,129},{129,193},{193,1... | collective-permute-start | bytes 49160 | tf_op jit(solution)/shard_map/ppermute | solution.py:29
  44.0 16.5 %collective-permute-start.20 = (bf16[64,128]{1,0:T(8,128)(2,1)S(1)}, bf16[64,128]{1,0:T(8,128)(2,1)S(1)}, u32[]{:S(2)}, u32[]{:S(2)}) collective-permute-start(bf16[64,128]{1,0:T(8,128)(2,1)S(1)} %add_convert_fusion.8.refs_6_), channel_id=1, source_target_pairs={{0,128},{64,192},{128,0},{192,64},{1,129},{65,193},{129,1},{193,65... | collective-permute-start | bytes 49160 | tf_op jit(solution)/shard_map/ppermute | solution.py:29
  47.3 13.2 %collective-permute-start.21 = (bf16[64,128]{1,0:T(8,128)(2,1)S(1)}, bf16[64,128]{1,0:T(8,128)(2,1)S(1)}, u32[]{:S(2)}, u32[]{:S(2)}) collective-permute-start(bf16[64,128]{1,0:T(8,128)(2,1)S(1)} %add_convert_fusion.8.refs_6_), channel_id=1, source_target_pairs={{0,192},{64,0},{128,64},{192,128},{1,193},{65,1},{129,65},{193,129... | collective-permute-start | bytes 49160 | tf_op jit(solution)/shard_map/ppermute | solution.py:29
  53.9 16.2 %collective-permute-start.10 = (bf16[512,128]{1,0:T(8,128)(2,1)S(1)}, bf16[512,128]{1,0:T(8,128)(2,1)S(1)}, u32[]{:S(2)}, u32[]{:S(2)}) collective-permute-start(bf16[512,128]{1,0:T(8,128)(2,1)S(1)} %get-tuple-element.63), channel_id=1, source_target_pairs={{0,16},{8,24},{16,32},{24,40},{32,48},{40,56},{48,0},{56,8},{1,17}... | collective-permute-start | bytes 393224 | tf_op jit(solution)/shard_map/ppermute | solution.py:29
  57.2 14.4 %collective-permute-start.9 = (bf16[512,128]{1,0:T(8,128)(2,1)S(1)}, bf16[512,128]{1,0:T(8,128)(2,1)S(1)}, u32[]{:S(2)}, u32[]{:S(2)}) collective-permute-start(bf16[512,128]{1,0:T(8,128)(2,1)S(1)} %get-tuple-element.61), channel_id=1, source_target_pairs={{0,8},{8,16},{16,24},{24,32},{32,40},{40,48},{48,56},{56,0},{1,9},... | collective-permute-start | bytes 393224 | tf_op jit(solution)/shard_map/ppermute | solution.py:29
  59.1 13.1 %collective-permute-start.13 = (bf16[512,128]{1,0:T(8,128)(2,1)S(1)}, bf16[512,128]{1,0:T(8,128)(2,1)S(1)}, u32[]{:S(2)}, u32[]{:S(2)}) collective-permute-start(bf16[512,128]{1,0:T(8,128)(2,1)S(1)} %get-tuple-element.65), channel_id=1, source_target_pairs={{0,56},{8,0},{16,8},{24,16},{32,24},{40,32},{48,40},{56,48},{1,57}... | collective-permute-start | bytes 393224 | tf_op jit(solution)/shard_map/ppermute | solution.py:29
  66.9 8.2 %collective-permute-start.22 = (bf16[528,128]{1,0:T(8,128)(2,1)S(1)}, bf16[528,128]{1,0:T(8,128)(2,1)S(1)}, u32[]{:S(2)}, u32[]{:S(2)}) collective-permute-start(bf16[528,128]{1,0:T(8,128)(2,1)S(1)} %get-tuple-element.73), channel_id=1, source_target_pairs={{0,8},{8,16},{16,24},{24,32},{32,40},{40,48},{48,56},{56,0},{1,9},... | collective-permute-start | bytes 405512 | tf_op jit(solution)/shard_map/ppermute | solution.py:29
  69.0 8.4 %collective-permute-start.26 = (bf16[528,128]{1,0:T(8,128)(2,1)S(1)}, bf16[528,128]{1,0:T(8,128)(2,1)S(1)}, u32[]{:S(2)}, u32[]{:S(2)}) collective-permute-start(bf16[528,128]{1,0:T(8,128)(2,1)S(1)} %get-tuple-element.78), channel_id=1, source_target_pairs={{0,48},{8,56},{16,0},{24,8},{32,16},{40,24},{48,32},{56,40},{1,49}... | collective-permute-start | bytes 405512 | tf_op jit(solution)/shard_map/ppermute | solution.py:29
  70.1 10.5 %collective-permute-start.25 = (bf16[528,128]{1,0:T(8,128)(2,1)S(1)}, bf16[528,128]{1,0:T(8,128)(2,1)S(1)}, u32[]{:S(2)}, u32[]{:S(2)}) collective-permute-start(bf16[528,128]{1,0:T(8,128)(2,1)S(1)} %get-tuple-element.76), channel_id=1, source_target_pairs={{0,56},{8,0},{16,8},{24,16},{32,24},{40,32},{48,40},{56,48},{1,57}... | collective-permute-start | bytes 405512 | tf_op jit(solution)/shard_map/ppermute | solution.py:29
  71.6 10.6 %collective-permute-start.11 = (bf16[512,128]{1,0:T(8,128)(2,1)S(1)}, bf16[512,128]{1,0:T(8,128)(2,1)S(1)}, u32[]{:S(2)}, u32[]{:S(2)}) collective-permute-start(bf16[512,128]{1,0:T(8,128)(2,1)S(1)} %add_convert_fusion.7), channel_id=1, source_target_pairs={{0,8},{8,16},{16,24},{24,32},{32,40},{40,48},{48,56},{56,0},{1,9},... | collective-permute-start | bytes 393224 | tf_op jit(solution)/shard_map/ppermute | solution.py:29
  72.3 17.7 %collective-permute-start.14 = (bf16[512,128]{1,0:T(8,128)(2,1)S(1)}, bf16[512,128]{1,0:T(8,128)(2,1)S(1)}, u32[]{:S(2)}, u32[]{:S(2)}) collective-permute-start(bf16[512,128]{1,0:T(8,128)(2,1)S(1)} %add_convert_fusion.5), channel_id=1, source_target_pairs={{0,56},{8,0},{16,8},{24,16},{32,24},{40,32},{48,40},{56,48},{1,57}... | collective-permute-start | bytes 393224 | tf_op jit(solution)/shard_map/ppermute | solution.py:29
  75.1 7.8 %collective-permute-start.23 = (bf16[528,128]{1,0:T(8,128)(2,1)S(1)}, bf16[528,128]{1,0:T(8,128)(2,1)S(1)}, u32[]{:S(2)}, u32[]{:S(2)}) collective-permute-start(bf16[528,128]{1,0:T(8,128)(2,1)S(1)} %add_convert_fusion.3), channel_id=1, source_target_pairs={{0,8},{8,16},{16,24},{24,32},{32,40},{40,48},{48,56},{56,0},{1,9},... | collective-permute-start | bytes 405512 | tf_op jit(solution)/shard_map/ppermute | solution.py:29
  80.7 6.5 %collective-permute-start.27 = (bf16[528,128]{1,0:T(8,128)(2,1)S(1)}, bf16[528,128]{1,0:T(8,128)(2,1)S(1)}, u32[]{:S(2)}, u32[]{:S(2)}) collective-permute-start(bf16[528,128]{1,0:T(8,128)(2,1)S(1)} %add_convert_fusion.1), channel_id=1, source_target_pairs={{0,56},{8,0},{16,8},{24,16},{32,24},{40,32},{48,40},{56,48},{1,57}... | collective-permute-start | bytes 405512 | tf_op jit(solution)/shard_map/ppermute | solution.py:29
  82.3 7.9 %collective-permute-start.12 = (bf16[512,128]{1,0:T(8,128)(2,1)S(1)}, bf16[512,128]{1,0:T(8,128)(2,1)S(1)}, u32[]{:S(2)}, u32[]{:S(2)}) collective-permute-start(bf16[512,128]{1,0:T(8,128)(2,1)S(1)} %add_convert_fusion.6), channel_id=1, source_target_pairs={{0,8},{8,16},{16,24},{24,32},{32,40},{40,48},{48,56},{56,0},{1,9},... | collective-permute-start | bytes 393224 | tf_op jit(solution)/shard_map/ppermute | solution.py:29
  83.0 12.3 %collective-permute-start.24 = (bf16[528,128]{1,0:T(8,128)(2,1)S(1)}, bf16[528,128]{1,0:T(8,128)(2,1)S(1)}, u32[]{:S(2)}, u32[]{:S(2)}) collective-permute-start(bf16[528,128]{1,0:T(8,128)(2,1)S(1)} %add_convert_fusion.2), channel_id=1, source_target_pairs={{0,8},{8,16},{16,24},{24,32},{32,40},{40,48},{48,56},{56,0},{1,9},... | collective-permute-start | bytes 405512 | tf_op jit(solution)/shard_map/ppermute | solution.py:29
  87.3 8.0 %collective-permute-start.28 = (bf16[528,128]{1,0:T(8,128)(2,1)S(1)}, bf16[528,128]{1,0:T(8,128)(2,1)S(1)}, u32[]{:S(2)}, u32[]{:S(2)}) collective-permute-start(bf16[528,128]{1,0:T(8,128)(2,1)S(1)} %add_convert_fusion), channel_id=1, source_target_pairs={{0,56},{8,0},{16,8},{24,16},{32,24},{40,32},{48,40},{56,48},{1,57}... | collective-permute-start | bytes 405512 | tf_op jit(solution)/shard_map/ppermute | solution.py:29
  90.1 5.0 %collective-permute-start.15 = (bf16[512,128]{1,0:T(8,128)(2,1)S(1)}, bf16[512,128]{1,0:T(8,128)(2,1)S(1)}, u32[]{:S(2)}, u32[]{:S(2)}) collective-permute-start(bf16[512,128]{1,0:T(8,128)(2,1)S(1)} %add_convert_fusion.4), channel_id=1, source_target_pairs={{0,56},{8,0},{16,8},{24,16},{32,24},{40,32},{48,40},{56,48},{1,57}... | collective-permute-start | bytes 393224 | tf_op jit(solution)/shard_map/ppermute | solution.py:29
